TPU v7x, 1024 devices: a whole 4x4x32 slice. The times are simulated.
1024 devices in a mesh: ctx: 128 (over x, y, z_lo), tp: 8 (over z_hi, core).
Axes of the slice: x: 4, y: 4, z: 32 (z_hi: 4, z_lo: 8; z = z_hi * 8 + z_lo), core: 2. Of those that a mesh axis runs over, the one named last changes fastest.
Arguments:
- queries: bfloat16 [2, 128, 128, 8192], P(None, 'ctx', None, 'tp'), may hold values from -5 to 5
- keys: bfloat16 [2, 128, 128, 1024], P(None, 'ctx', None, 'tp'), may hold values from -5 to 5
- values: bfloat16 [2, 128, 128, 1024], P(None, 'ctx', None, 'tp'), may hold values from -6 to 6
- out_grad: bfloat16 [2, 128, 128, 8192], P(None, 'ctx', None, 'tp'), may hold values from -6 to 6
- block_doc: int32 [256], replicated, may hold values from 0 to 255, as said below
Outputs:
- attn_out: bfloat16 [2, 128, 128, 8192], P(None, 'ctx', None, 'tp')
- query_grad: bfloat16 [2, 128, 128, 8192], P(None, 'ctx', None, 'tp')
- key_grad: bfloat16 [2, 128, 128, 1024], P(None, 'ctx', None, 'tp')
- value_grad: bfloat16 [2, 128, 128, 1024], P(None, 'ctx', None, 'tp')
Inputs may be any that keep to these rules, and one draw needn't show every extreme that they name: block_doc never falls along the sequence; each document covers 1 to 8 consecutive blocks, and in each half of the sequence the first document covers exactly 8; no document holds both block 127 and block 128; the first block's id is 0 and the last block's id is 255.
All inputs are finite; a program needn't handle non-finite values.
Results may differ from a plain program's by a relative error of at most 0.0094.
Values may be sent and summed in bfloat16 or wider, within the bound.
A program may use at most 32 MiB of HBM per device.

v0:
```python
import math

import jax
import jax.numpy as jnp
from jax import lax
from jax.sharding import PartitionSpec as P

HQ = 64
HK = 8
HD = 128
BLOCK = 128


masked_score = -1e30


def shifted(block, axis, distance):
    devices = range(lax.axis_size(axis))
    route = [(i - distance, i) for i in devices if i - distance in devices]
    return lax.ppermute(block, axis, route)


def move_keys(payload, distance):
    return shifted(payload, "ctx", distance)


def move_grads(payload, distance):
    return shifted(payload.astype(jnp.bfloat16), "ctx", distance).astype(payload.dtype)


def piece_docs(block_doc, piece_index, piece_len):
    per_piece = piece_len // BLOCK
    start = jnp.maximum(piece_index, 0) * per_piece
    doc_blocks = lax.dynamic_slice_in_dim(block_doc, start, per_piece, 0)
    doc_tokens = jnp.repeat(doc_blocks, BLOCK)
    return jnp.where(piece_index >= 0, doc_tokens, -1)


def attend(query_piece, grad_piece, key_buffer, piece_index, block_doc):
    window, _, piece_len, features = key_buffer.shape
    kv_heads = features // HD
    scaling = 1.0 / math.sqrt(HD)
    key_slots = key_buffer[:, 0].reshape(window, piece_len, kv_heads, HD)
    value_slots = key_buffer[:, 1].reshape(window, piece_len, kv_heads, HD)
    keys_flat = key_slots.reshape(window * piece_len, kv_heads, HD)
    values_flat = value_slots.reshape(window * piece_len, kv_heads, HD)
    positions = jnp.arange(piece_len, dtype=jnp.int32)
    query_docs = piece_docs(block_doc, piece_index, piece_len)
    query_pos = piece_index * piece_len + positions
    visible_rows = []
    for slot_index in range(window):
        key_index = piece_index - (window - 1) + slot_index
        key_docs = piece_docs(block_doc, key_index, piece_len)
        key_pos = key_index * piece_len + positions
        visible_rows.append(
            (key_docs[None, :] == query_docs[:, None]) & (key_pos[None, :] <= query_pos[:, None])
        )
    visible = jnp.concatenate(visible_rows, axis=1)

    def key_side(form, left, flat):
        return jnp.einsum(form, left, flat, preferred_element_type=jnp.float32)

    def key_sum(form, weights, flat):
        return jnp.einsum(form, weights, flat, preferred_element_type=jnp.float32)

    def per_key(form, weights, right):
        return jnp.einsum(form, weights, right, preferred_element_type=jnp.float32).reshape(
            window, piece_len, kv_heads, HD
        )

    raw_scores = key_side("qhgd,khd->hgqk", query_piece, keys_flat)
    scores = jnp.where(visible[None, None], raw_scores * scaling, masked_score)
    row_max = jnp.max(scores, axis=-1, keepdims=True)
    log_total = row_max + jnp.log(jnp.sum(jnp.exp(scores - row_max), axis=-1, keepdims=True))
    probs = jnp.exp(scores - log_total)
    probs_low = probs.astype(jnp.bfloat16)
    attended = key_sum("hgqk,khd->qhgd", probs_low, values_flat)
    out_low = attended.astype(jnp.bfloat16)
    out_back = lax.optimization_barrier(out_low).astype(jnp.float32)
    delta = jnp.einsum("qhgd,qhgd->hgq", grad_piece.astype(jnp.float32), out_back)
    dprobs = key_side("qhgd,khd->hgqk", grad_piece, values_flat)
    dscores = (probs * (dprobs - delta[..., None])).astype(jnp.bfloat16)
    query_part = (key_sum("hgqk,khd->qhgd", dscores, keys_flat) * scaling).astype(jnp.bfloat16)
    key_part = per_key("hgqk,qhgd->khd", dscores, query_piece) * scaling
    value_part = per_key("hgqk,qhgd->khd", probs_low, grad_piece)
    grads = jnp.stack(
        [
            key_part.reshape(window, piece_len, features),
            value_part.reshape(window, piece_len, features),
        ],
        axis=1,
    )
    return (out_low.reshape(piece_len, -1), query_part.reshape(piece_len, -1), grads)


def local(queries, keys, values, out_grad, block_doc):
    ctx_size = lax.axis_size("ctx")
    my_index = lax.axis_index("ctx")
    reach_back = min(7, ctx_size // 4 - 1)
    window = reach_back + 1
    piece_len = queries.shape[2]
    kv_heads = keys.shape[3] // HD
    group = HQ // HK
    query_all = queries[:, 0].reshape(2, piece_len, kv_heads, group, HD)
    grad_all = out_grad[:, 0].reshape(2, piece_len, kv_heads, group, HD)
    paired = jnp.stack([keys[:, 0], values[:, 0]], axis=1)
    low_buffer = jnp.stack(
        [move_keys(paired[0], window - 1 - slot_index) for slot_index in range(window - 1)]
        + [paired[0]]
    )
    high_buffer = jnp.stack(
        [move_keys(paired[1], -(window - 1 - slot_index)) for slot_index in range(window - 1)]
        + [paired[1]]
    )
    high_index = 2 * ctx_size - 1 - my_index
    low_out, low_qgrad, low_grads = attend(
        query_all[0], grad_all[0], low_buffer, my_index, block_doc
    )
    high_out, high_qgrad, high_grads = attend(
        query_all[1], grad_all[1], high_buffer, high_index, block_doc
    )
    low_total = low_grads[window - 1]
    high_total = high_grads[window - 1]
    for distance in range(1, window):
        low_total = low_total + move_grads(low_grads[window - 1 - distance], -distance)
        high_total = high_total + move_grads(high_grads[window - 1 - distance], distance)
    attn_pair = jnp.stack([low_out, high_out])[:, None]
    qgrad_pair = jnp.stack([low_qgrad, high_qgrad])[:, None]
    key_pair = jnp.stack([low_total[0], high_total[0]]).astype(jnp.bfloat16)[:, None]
    value_pair = jnp.stack([low_total[1], high_total[1]]).astype(jnp.bfloat16)[:, None]
    return (attn_pair, qgrad_pair, key_pair, value_pair)


def solution(mesh):
    in_specs = (
        P(None, "ctx", None, "tp"),
        P(None, "ctx", None, "tp"),
        P(None, "ctx", None, "tp"),
        P(None, "ctx", None, "tp"),
        P(),
    )
    out_specs = (
        P(None, "ctx", None, "tp"),
        P(None, "ctx", None, "tp"),
        P(None, "ctx", None, "tp"),
        P(None, "ctx", None, "tp"),
    )
    return jax.shard_map(local, mesh=mesh, in_specs=in_specs, out_specs=out_specs, check_vma=False)
```

profile of v0, /device:TPU:728, one launch (start us, length us, event | category | flops | bytes accessed | tf_op | source)
XLA Modules:
  0.0 253.1 jit_solution(5878373309133981993)
XLA Ops:
  2.3 2.9 %collective-permute-start.6 = (bf16[2,128,128]{2,1,0:T(8,128)(2,1)S(1)}, bf16[2,128,128]{2,1,0:T(8,128)(2,1)S(1)}, u32[]{:S(2)}, u32[]{:S(2)}) collective-permute-start(bf16[2,128,128]{2,1,0:T(8,128)(2,1)S(1)} %get-tuple-element.28), channel_id=1, source_target_pairs={{0,8},{8,16},{16,24},{24,32},{32,40},{40,48},{48,56},{56,64},{64,7... | collective-permute-start | bytes 196616 | tf_op jit(solution)/shard_map/ppermute | solution.py:20
  5.3 6.9 %collective-permute-start.5 = (bf16[2,128,128]{2,1,0:T(8,128)(2,1)S(1)}, bf16[2,128,128]{2,1,0:T(8,128)(2,1)S(1)}, u32[]{:S(2)}, u32[]{:S(2)}) collective-permute-start(bf16[2,128,128]{2,1,0:T(8,128)(2,1)S(1)} %get-tuple-element.28), channel_id=1, source_target_pairs={{0,16},{8,24},{16,32},{24,40},{32,48},{40,56},{48,64},{56,72},{64,... | collective-permute-start | bytes 196616 | tf_op jit(solution)/shard_map/ppermute | solution.py:20
  12.2 2.9 %collective-permute-start.4 = (bf16[2,128,128]{2,1,0:T(8,128)(2,1)S(1)}, bf16[2,128,128]{2,1,0:T(8,128)(2,1)S(1)}, u32[]{:S(2)}, u32[]{:S(2)}) collective-permute-start(bf16[2,128,128]{2,1,0:T(8,128)(2,1)S(1)} %get-tuple-element.28), channel_id=1, source_target_pairs={{0,24},{8,32},{16,40},{24,48},{32,56},{40,64},{48,72},{56,80},{64,... | collective-permute-start | bytes 196616 | tf_op jit(solution)/shard_map/ppermute | solution.py:20
  15.2 8.3 %collective-permute-start.3 = (bf16[2,128,128]{2,1,0:T(8,128)(2,1)S(1)}, bf16[2,128,128]{2,1,0:T(8,128)(2,1)S(1)}, u32[]{:S(2)}, u32[]{:S(2)}) collective-permute-start(bf16[2,128,128]{2,1,0:T(8,128)(2,1)S(1)} %get-tuple-element.28), channel_id=1, source_target_pairs={{0,32},{8,40},{16,48},{24,56},{32,64},{40,72},{48,80},{56,88},{64,... | collective-permute-start | bytes 196616 | tf_op jit(solution)/shard_map/ppermute | solution.py:20
  25.6 2.0 fusion.76
  42.4 6.9 %collective-permute-start = (bf16[2,128,128]{2,1,0:T(8,128)(2,1)S(1)}, bf16[2,128,128]{2,1,0:T(8,128)(2,1)S(1)}, u32[]{:S(2)}, u32[]{:S(2)}) collective-permute-start(bf16[2,128,128]{2,1,0:T(8,128)(2,1)S(1)} %get-tuple-element.28), channel_id=1, source_target_pairs={{0,56},{8,64},{16,72},{24,80},{32,88},{40,96},{48,104},{56,112},{6... | collective-permute-start | bytes 196616 | tf_op jit(solution)/shard_map/ppermute | solution.py:20
  51.2 6.9 %collective-permute-start.8 = (bf16[2,128,128]{2,1,0:T(8,128)(2,1)S(1)}, bf16[2,128,128]{2,1,0:T(8,128)(2,1)S(1)}, u32[]{:S(2)}, u32[]{:S(2)}) collective-permute-start(bf16[2,128,128]{2,1,0:T(8,128)(2,1)S(1)} %get-tuple-element.29), channel_id=1, source_target_pairs={{48,0},{56,8},{64,16},{72,24},{80,32},{88,40},{96,48},{104,56},{11... | collective-permute-start | bytes 196616 | tf_op jit(solution)/shard_map/ppermute | solution.py:20
  58.1 3.2 %collective-permute-done.8 = bf16[2,128,128]{2,1,0:T(8,128)(2,1)S(1)} collective-permute-done((bf16[2,128,128]{2,1,0:T(8,128)(2,1)S(1)}, bf16[2,128,128]{2,1,0:T(8,128)(2,1)S(1)}, u32[]{:S(2)}, u32[]{:S(2)}) %collective-permute-start.8) | collective-permute-done | bytes 65568 | tf_op jit(solution)/shard_map/ppermute | solution.py:20
  61.3 9.0 %collective-permute-start.9 = (bf16[2,128,128]{2,1,0:T(8,128)(2,1)S(1)}, bf16[2,128,128]{2,1,0:T(8,128)(2,1)S(1)}, u32[]{:S(2)}, u32[]{:S(2)}) collective-permute-start(bf16[2,128,128]{2,1,0:T(8,128)(2,1)S(1)} %get-tuple-element.29), channel_id=1, source_target_pairs={{40,0},{48,8},{56,16},{64,24},{72,32},{80,40},{88,48},{96,56},{104... | collective-permute-start | bytes 196616 | tf_op jit(solution)/shard_map/ppermute | solution.py:20
  70.3 3.8 %collective-permute-done.9 = bf16[2,128,128]{2,1,0:T(8,128)(2,1)S(1)} collective-permute-done((bf16[2,128,128]{2,1,0:T(8,128)(2,1)S(1)}, bf16[2,128,128]{2,1,0:T(8,128)(2,1)S(1)}, u32[]{:S(2)}, u32[]{:S(2)}) %collective-permute-start.9) | collective-permute-done | bytes 65568 | tf_op jit(solution)/shard_map/ppermute | solution.py:20
  74.1 5.4 %collective-permute-start.10 = (bf16[2,128,128]{2,1,0:T(8,128)(2,1)S(1)}, bf16[2,128,128]{2,1,0:T(8,128)(2,1)S(1)}, u32[]{:S(2)}, u32[]{:S(2)}) collective-permute-start(bf16[2,128,128]{2,1,0:T(8,128)(2,1)S(1)} %get-tuple-element.29), channel_id=1, source_target_pairs={{32,0},{40,8},{48,16},{56,24},{64,32},{72,40},{80,48},{88,56},{96,... | collective-permute-start | bytes 196616 | tf_op jit(solution)/shard_map/ppermute | solution.py:20
  79.6 8.2 %collective-permute-done.10 = bf16[2,128,128]{2,1,0:T(8,128)(2,1)S(1)} collective-permute-done((bf16[2,128,128]{2,1,0:T(8,128)(2,1)S(1)}, bf16[2,128,128]{2,1,0:T(8,128)(2,1)S(1)}, u32[]{:S(2)}, u32[]{:S(2)}) %collective-permute-start.10) | collective-permute-done | bytes 65568 | tf_op jit(solution)/shard_map/ppermute | solution.py:20
  89.7 12.0 %collective-permute-done.11 = bf16[2,128,128]{2,1,0:T(8,128)(2,1)S(1)} collective-permute-done((bf16[2,128,128]{2,1,0:T(8,128)(2,1)S(1)}, bf16[2,128,128]{2,1,0:T(8,128)(2,1)S(1)}, u32[]{:S(2)}, u32[]{:S(2)}) %collective-permute-start.11) | collective-permute-done | bytes 65568 | tf_op jit(solution)/shard_map/ppermute | solution.py:20
  103.7 12.9 %collective-permute-done.12 = bf16[2,128,128]{2,1,0:T(8,128)(2,1)S(1)} collective-permute-done((bf16[2,128,128]{2,1,0:T(8,128)(2,1)S(1)}, bf16[2,128,128]{2,1,0:T(8,128)(2,1)S(1)}, u32[]{:S(2)}, u32[]{:S(2)}) %collective-permute-start.12) | collective-permute-done | bytes 65568 | tf_op jit(solution)/shard_map/ppermute | solution.py:20
  118.5 6.5 %collective-permute-done.13 = bf16[2,128,128]{2,1,0:T(8,128)(2,1)S(1)} collective-permute-done((bf16[2,128,128]{2,1,0:T(8,128)(2,1)S(1)}, bf16[2,128,128]{2,1,0:T(8,128)(2,1)S(1)}, u32[]{:S(2)}, u32[]{:S(2)}) %collective-permute-start.13) | collective-permute-done | bytes 65568 | tf_op jit(solution)/shard_map/ppermute | solution.py:20
  127.0 10.0 %collective-permute-done.1 = bf16[2,128,128]{2,1,0:T(8,128)(2,1)S(1)} collective-permute-done((bf16[2,128,128]{2,1,0:T(8,128)(2,1)S(1)}, bf16[2,128,128]{2,1,0:T(8,128)(2,1)S(1)}, u32[]{:S(2)}, u32[]{:S(2)}) %collective-permute-start.1) | collective-permute-done | bytes 65568 | tf_op jit(solution)/shard_map/ppermute | solution.py:20
  137.0 2.1 collective-permute-start.2
  139.1 11.9 %collective-permute-done.2 = bf16[2,128,128]{2,1,0:T(8,128)(2,1)S(1)} collective-permute-done((bf16[2,128,128]{2,1,0:T(8,128)(2,1)S(1)}, bf16[2,128,128]{2,1,0:T(8,128)(2,1)S(1)}, u32[]{:S(2)}, u32[]{:S(2)}) %collective-permute-start.2) | collective-permute-done | bytes 65568 | tf_op jit(solution)/shard_map/ppermute | solution.py:20
  166.0 10.6 %collective-permute-start.21 = (bf16[2,128,128]{2,1,0:T(8,128)(2,1)}, bf16[2,128,128]{2,1,0:T(8,128)(2,1)}, u32[]{:S(2)}, u32[]{:S(2)}) collective-permute-start(bf16[2,128,128]{2,1,0:T(8,128)(2,1)} %get-tuple-element.11), channel_id=1, source_target_pairs={{0,8},{8,16},{16,24},{24,32},{32,40},{40,48},{48,56},{56,64},{64,7... | collective-permute-start | bytes 196616 | tf_op jit(solution)/shard_map/ppermute | solution.py:20
  176.5 1.9 collective-permute-start.27
  178.5 1.9 collective-permute-start.26
  180.4 3.1 %collective-permute-start.25 = (bf16[2,128,128]{2,1,0:T(8,128)(2,1)}, bf16[2,128,128]{2,1,0:T(8,128)(2,1)}, u32[]{:S(2)}, u32[]{:S(2)}) collective-permute-start(bf16[2,128,128]{2,1,0:T(8,128)(2,1)} %get-tuple-element.14), channel_id=1, source_target_pairs={{0,40},{8,48},{16,56},{24,64},{32,72},{40,80},{48,88},{56,96},{64,... | collective-permute-start | bytes 196616 | tf_op jit(solution)/shard_map/ppermute | solution.py:20
  183.5 2.9 %collective-permute-start.24 = (bf16[2,128,128]{2,1,0:T(8,128)(2,1)}, bf16[2,128,128]{2,1,0:T(8,128)(2,1)}, u32[]{:S(2)}, u32[]{:S(2)}) collective-permute-start(bf16[2,128,128]{2,1,0:T(8,128)(2,1)} %get-tuple-element.15), channel_id=1, source_target_pairs={{0,32},{8,40},{16,48},{24,56},{32,64},{40,72},{48,80},{56,88},{64,... | collective-permute-start | bytes 196616 | tf_op jit(solution)/shard_map/ppermute | solution.py:20
  189.4 5.4 %collective-permute-start.23 = (bf16[2,128,128]{2,1,0:T(8,128)(2,1)S(1)}, bf16[2,128,128]{2,1,0:T(8,128)(2,1)S(1)}, u32[]{:S(2)}, u32[]{:S(2)}) collective-permute-start(bf16[2,128,128]{2,1,0:T(8,128)(2,1)S(1)} %get-tuple-element.16), channel_id=1, source_target_pairs={{0,24},{8,32},{16,40},{24,48},{32,56},{40,64},{48,72},{56,80},{64,... | collective-permute-start | bytes 196616 | tf_op jit(solution)/shard_map/ppermute | solution.py:20
  194.8 9.4 %collective-permute-start.22 = (bf16[2,128,128]{2,1,0:T(8,128)(2,1)S(1)}, bf16[2,128,128]{2,1,0:T(8,128)(2,1)S(1)}, u32[]{:S(2)}, u32[]{:S(2)}) collective-permute-start(bf16[2,128,128]{2,1,0:T(8,128)(2,1)S(1)} %get-tuple-element.17), channel_id=1, source_target_pairs={{0,16},{8,24},{16,32},{24,40},{32,48},{40,56},{48,64},{56,72},{64,... | collective-permute-start | bytes 196616 | tf_op jit(solution)/shard_map/ppermute | solution.py:20
  209.0 6.1 %collective-permute-start.19 = (bf16[2,128,128]{2,1,0:T(8,128)(2,1)S(1)}, bf16[2,128,128]{2,1,0:T(8,128)(2,1)S(1)}, u32[]{:S(2)}, u32[]{:S(2)}) collective-permute-start(bf16[2,128,128]{2,1,0:T(8,128)(2,1)S(1)} %get-tuple-element.6), channel_id=1, source_target_pairs={{48,0},{56,8},{64,16},{72,24},{80,32},{88,40},{96,48},{104,56},{11... | collective-permute-start | bytes 196616 | tf_op jit(solution)/shard_map/ppermute | solution.py:20
  215.1 8.1 %collective-permute-start.18 = (bf16[2,128,128]{2,1,0:T(8,128)(2,1)S(1)}, bf16[2,128,128]{2,1,0:T(8,128)(2,1)S(1)}, u32[]{:S(2)}, u32[]{:S(2)}) collective-permute-start(bf16[2,128,128]{2,1,0:T(8,128)(2,1)S(1)} %get-tuple-element.7), channel_id=1, source_target_pairs={{40,0},{48,8},{56,16},{64,24},{72,32},{80,40},{88,48},{96,56},{104... | collective-permute-start | bytes 196616 | tf_op jit(solution)/shard_map/ppermute | solution.py:20
  223.3 10.6 %collective-permute-start.17 = (bf16[2,128,128]{2,1,0:T(8,128)(2,1)S(1)}, bf16[2,128,128]{2,1,0:T(8,128)(2,1)S(1)}, u32[]{:S(2)}, u32[]{:S(2)}) collective-permute-start(bf16[2,128,128]{2,1,0:T(8,128)(2,1)S(1)} %get-tuple-element.8), channel_id=1, source_target_pairs={{32,0},{40,8},{48,16},{56,24},{64,32},{72,40},{80,48},{88,56},{96,... | collective-permute-start | bytes 196616 | tf_op jit(solution)/shard_map/ppermute | solution.py:20
  234.9 1.9 collective-permute-start.16
  236.8 3.4 %collective-permute-start.15 = (bf16[2,128,128]{2,1,0:T(8,128)(2,1)S(1)}, bf16[2,128,128]{2,1,0:T(8,128)(2,1)S(1)}, u32[]{:S(2)}, u32[]{:S(2)}) collective-permute-start(bf16[2,128,128]{2,1,0:T(8,128)(2,1)S(1)} %get-tuple-element.10), channel_id=1, source_target_pairs={{16,0},{24,8},{32,16},{40,24},{48,32},{56,40},{64,48},{72,56},{80,... | collective-permute-start | bytes 196616 | tf_op jit(solution)/shard_map/ppermute | solution.py:20
  240.2 8.6 %collective-permute-done.16 = bf16[2,128,128]{2,1,0:T(8,128)(2,1)S(1)} collective-permute-done((bf16[2,128,128]{2,1,0:T(8,128)(2,1)S(1)}, bf16[2,128,128]{2,1,0:T(8,128)(2,1)S(1)}, u32[]{:S(2)}, u32[]{:S(2)}) %collective-permute-start.16) | collective-permute-done | bytes 65568 | tf_op jit(solution)/shard_map/ppermute | solution.py:20
  248.9 2.8 %collective-permute-done.15 = bf16[2,128,128]{2,1,0:T(8,128)(2,1)S(1)} collective-permute-done((bf16[2,128,128]{2,1,0:T(8,128)(2,1)S(1)}, bf16[2,128,128]{2,1,0:T(8,128)(2,1)S(1)}, u32[]{:S(2)}, u32[]{:S(2)}) %collective-permute-start.15) | collective-permute-done | bytes 65568 | tf_op jit(solution)/shard_map/ppermute | solution.py:20
  (116 shorter events, 42.4 us)
Async XLA Ops:
  2.3 148.8 %collective-permute-start.6 = (bf16[2,128,128]{2,1,0:T(8,128)(2,1)S(1)}, bf16[2,128,128]{2,1,0:T(8,128)(2,1)S(1)}, u32[]{:S(2)}, u32[]{:S(2)}) collective-permute-start(bf16[2,128,128]{2,1,0:T(8,128)(2,1)S(1)} %get-tuple-element.28), channel_id=1, source_target_pairs={{0,8},{8,16},{16,24},{24,32},{32,40},{40,48},{48,56},{56,64},{64,7... | collective-permute-start | bytes 196616 | tf_op jit(solution)/shard_map/ppermute | solution.py:20
  5.3 145.8 %collective-permute-start.5 = (bf16[2,128,128]{2,1,0:T(8,128)(2,1)S(1)}, bf16[2,128,128]{2,1,0:T(8,128)(2,1)S(1)}, u32[]{:S(2)}, u32[]{:S(2)}) collective-permute-start(bf16[2,128,128]{2,1,0:T(8,128)(2,1)S(1)} %get-tuple-element.28), channel_id=1, source_target_pairs={{0,16},{8,24},{16,32},{24,40},{32,48},{40,56},{48,64},{56,72},{64,... | collective-permute-start | bytes 196616 | tf_op jit(solution)/shard_map/ppermute | solution.py:20
  12.2 138.8 %collective-permute-start.4 = (bf16[2,128,128]{2,1,0:T(8,128)(2,1)S(1)}, bf16[2,128,128]{2,1,0:T(8,128)(2,1)S(1)}, u32[]{:S(2)}, u32[]{:S(2)}) collective-permute-start(bf16[2,128,128]{2,1,0:T(8,128)(2,1)S(1)} %get-tuple-element.28), channel_id=1, source_target_pairs={{0,24},{8,32},{16,40},{24,48},{32,56},{40,64},{48,72},{56,80},{64,... | collective-permute-start | bytes 196616 | tf_op jit(solution)/shard_map/ppermute | solution.py:20
  15.2 135.8 %collective-permute-start.3 = (bf16[2,128,128]{2,1,0:T(8,128)(2,1)S(1)}, bf16[2,128,128]{2,1,0:T(8,128)(2,1)S(1)}, u32[]{:S(2)}, u32[]{:S(2)}) collective-permute-start(bf16[2,128,128]{2,1,0:T(8,128)(2,1)S(1)} %get-tuple-element.28), channel_id=1, source_target_pairs={{0,32},{8,40},{16,48},{24,56},{32,64},{40,72},{48,80},{56,88},{64,... | collective-permute-start | bytes 196616 | tf_op jit(solution)/shard_map/ppermute | solution.py:20
  23.4 18.9 %collective-permute-start.7 = (bf16[2,128,128]{2,1,0:T(8,128)(2,1)S(1)}, bf16[2,128,128]{2,1,0:T(8,128)(2,1)S(1)}, u32[]{:S(2)}, u32[]{:S(2)}) collective-permute-start(bf16[2,128,128]{2,1,0:T(8,128)(2,1)S(1)} %get-tuple-element.29), channel_id=1, source_target_pairs={{56,0},{64,8},{72,16},{80,24},{88,32},{96,40},{104,48},{112,56},{1... | collective-permute-start | bytes 196616 | tf_op jit(solution)/shard_map/ppermute | solution.py:20
  42.4 8.8 %collective-permute-start = (bf16[2,128,128]{2,1,0:T(8,128)(2,1)S(1)}, bf16[2,128,128]{2,1,0:T(8,128)(2,1)S(1)}, u32[]{:S(2)}, u32[]{:S(2)}) collective-permute-start(bf16[2,128,128]{2,1,0:T(8,128)(2,1)S(1)} %get-tuple-element.28), channel_id=1, source_target_pairs={{0,56},{8,64},{16,72},{24,80},{32,88},{40,96},{48,104},{56,112},{6... | collective-permute-start | bytes 196616 | tf_op jit(solution)/shard_map/ppermute | solution.py:20
  51.2 10.1 %collective-permute-start.8 = (bf16[2,128,128]{2,1,0:T(8,128)(2,1)S(1)}, bf16[2,128,128]{2,1,0:T(8,128)(2,1)S(1)}, u32[]{:S(2)}, u32[]{:S(2)}) collective-permute-start(bf16[2,128,128]{2,1,0:T(8,128)(2,1)S(1)} %get-tuple-element.29), channel_id=1, source_target_pairs={{48,0},{56,8},{64,16},{72,24},{80,32},{88,40},{96,48},{104,56},{11... | collective-permute-start | bytes 196616 | tf_op jit(solution)/shard_map/ppermute | solution.py:20
  61.3 12.9 %collective-permute-start.9 = (bf16[2,128,128]{2,1,0:T(8,128)(2,1)S(1)}, bf16[2,128,128]{2,1,0:T(8,128)(2,1)S(1)}, u32[]{:S(2)}, u32[]{:S(2)}) collective-permute-start(bf16[2,128,128]{2,1,0:T(8,128)(2,1)S(1)} %get-tuple-element.29), channel_id=1, source_target_pairs={{40,0},{48,8},{56,16},{64,24},{72,32},{80,40},{88,48},{96,56},{104... | collective-permute-start | bytes 196616 | tf_op jit(solution)/shard_map/ppermute | solution.py:20
  74.1 13.6 %collective-permute-start.10 = (bf16[2,128,128]{2,1,0:T(8,128)(2,1)S(1)}, bf16[2,128,128]{2,1,0:T(8,128)(2,1)S(1)}, u32[]{:S(2)}, u32[]{:S(2)}) collective-permute-start(bf16[2,128,128]{2,1,0:T(8,128)(2,1)S(1)} %get-tuple-element.29), channel_id=1, source_target_pairs={{32,0},{40,8},{48,16},{56,24},{64,32},{72,40},{80,48},{88,56},{96,... | collective-permute-start | bytes 196616 | tf_op jit(solution)/shard_map/ppermute | solution.py:20
  87.8 14.0 %collective-permute-start.11 = (bf16[2,128,128]{2,1,0:T(8,128)(2,1)S(1)}, bf16[2,128,128]{2,1,0:T(8,128)(2,1)S(1)}, u32[]{:S(2)}, u32[]{:S(2)}) collective-permute-start(bf16[2,128,128]{2,1,0:T(8,128)(2,1)S(1)} %get-tuple-element.29), channel_id=1, source_target_pairs={{24,0},{32,8},{40,16},{48,24},{56,32},{64,40},{72,48},{80,56},{88,... | collective-permute-start | bytes 196616 | tf_op jit(solution)/shard_map/ppermute | solution.py:20
  101.7 14.9 %collective-permute-start.12 = (bf16[2,128,128]{2,1,0:T(8,128)(2,1)S(1)}, bf16[2,128,128]{2,1,0:T(8,128)(2,1)S(1)}, u32[]{:S(2)}, u32[]{:S(2)}) collective-permute-start(bf16[2,128,128]{2,1,0:T(8,128)(2,1)S(1)} %get-tuple-element.29), channel_id=1, source_target_pairs={{16,0},{24,8},{32,16},{40,24},{48,32},{56,40},{64,48},{72,56},{80,... | collective-permute-start | bytes 196616 | tf_op jit(solution)/shard_map/ppermute | solution.py:20
  116.6 8.5 %collective-permute-start.13 = (bf16[2,128,128]{2,1,0:T(8,128)(2,1)S(1)}, bf16[2,128,128]{2,1,0:T(8,128)(2,1)S(1)}, u32[]{:S(2)}, u32[]{:S(2)}) collective-permute-start(bf16[2,128,128]{2,1,0:T(8,128)(2,1)S(1)} %get-tuple-element.29), channel_id=1, source_target_pairs={{8,0},{16,8},{24,16},{32,24},{40,32},{48,40},{56,48},{64,56},{72,6... | collective-permute-start | bytes 196616 | tf_op jit(solution)/shard_map/ppermute | solution.py:20
  125.0 12.0 %collective-permute-start.1 = (bf16[2,128,128]{2,1,0:T(8,128)(2,1)S(1)}, bf16[2,128,128]{2,1,0:T(8,128)(2,1)S(1)}, u32[]{:S(2)}, u32[]{:S(2)}) collective-permute-start(bf16[2,128,128]{2,1,0:T(8,128)(2,1)S(1)} %get-tuple-element.28), channel_id=1, source_target_pairs={{0,48},{8,56},{16,64},{24,72},{32,80},{40,88},{48,96},{56,104},{64... | collective-permute-start | bytes 196616 | tf_op jit(solution)/shard_map/ppermute | solution.py:20
  137.0 14.0 %collective-permute-start.2 = (bf16[2,128,128]{2,1,0:T(8,128)(2,1)S(1)}, bf16[2,128,128]{2,1,0:T(8,128)(2,1)S(1)}, u32[]{:S(2)}, u32[]{:S(2)}) collective-permute-start(bf16[2,128,128]{2,1,0:T(8,128)(2,1)S(1)} %get-tuple-element.28), channel_id=1, source_target_pairs={{0,40},{8,48},{16,56},{24,64},{32,72},{40,80},{48,88},{56,96},{64,... | collective-permute-start | bytes 196616 | tf_op jit(solution)/shard_map/ppermute | solution.py:20
  165.0 22.5 %copy-start = (bf16[1,128,1024]{2,1,0:T(8,128)(2,1)S(1)}, bf16[1,128,1024]{2,1,0:T(8,128)(2,1)}, u32[]{:S(2)}) copy-start(bf16[1,128,1024]{2,1,0:T(8,128)(2,1)} %copy.36) | copy-start | bytes 786436
  166.0 23.4 %collective-permute-start.21 = (bf16[2,128,128]{2,1,0:T(8,128)(2,1)}, bf16[2,128,128]{2,1,0:T(8,128)(2,1)}, u32[]{:S(2)}, u32[]{:S(2)}) collective-permute-start(bf16[2,128,128]{2,1,0:T(8,128)(2,1)} %get-tuple-element.11), channel_id=1, source_target_pairs={{0,8},{8,16},{16,24},{24,32},{32,40},{40,48},{48,56},{56,64},{64,7... | collective-permute-start | bytes 196616 | tf_op jit(solution)/shard_map/ppermute | solution.py:20
  176.5 18.3 %collective-permute-start.27 = (bf16[2,128,128]{2,1,0:T(8,128)(2,1)}, bf16[2,128,128]{2,1,0:T(8,128)(2,1)}, u32[]{:S(2)}, u32[]{:S(2)}) collective-permute-start(bf16[2,128,128]{2,1,0:T(8,128)(2,1)} %get-tuple-element.12), channel_id=1, source_target_pairs={{0,56},{8,64},{16,72},{24,80},{32,88},{40,96},{48,104},{56,112},{6... | collective-permute-start | bytes 196616 | tf_op jit(solution)/shard_map/ppermute | solution.py:20
  178.5 26.6 %collective-permute-start.26 = (bf16[2,128,128]{2,1,0:T(8,128)(2,1)}, bf16[2,128,128]{2,1,0:T(8,128)(2,1)}, u32[]{:S(2)}, u32[]{:S(2)}) collective-permute-start(bf16[2,128,128]{2,1,0:T(8,128)(2,1)} %get-tuple-element.13), channel_id=1, source_target_pairs={{0,48},{8,56},{16,64},{24,72},{32,80},{40,88},{48,96},{56,104},{64... | collective-permute-start | bytes 196616 | tf_op jit(solution)/shard_map/ppermute | solution.py:20
  180.4 26.6 %collective-permute-start.25 = (bf16[2,128,128]{2,1,0:T(8,128)(2,1)}, bf16[2,128,128]{2,1,0:T(8,128)(2,1)}, u32[]{:S(2)}, u32[]{:S(2)}) collective-permute-start(bf16[2,128,128]{2,1,0:T(8,128)(2,1)} %get-tuple-element.14), channel_id=1, source_target_pairs={{0,40},{8,48},{16,56},{24,64},{32,72},{40,80},{48,88},{56,96},{64,... | collective-permute-start | bytes 196616 | tf_op jit(solution)/shard_map/ppermute | solution.py:20
  183.5 25.4 %collective-permute-start.24 = (bf16[2,128,128]{2,1,0:T(8,128)(2,1)}, bf16[2,128,128]{2,1,0:T(8,128)(2,1)}, u32[]{:S(2)}, u32[]{:S(2)}) collective-permute-start(bf16[2,128,128]{2,1,0:T(8,128)(2,1)} %get-tuple-element.15), channel_id=1, source_target_pairs={{0,32},{8,40},{16,48},{24,56},{32,64},{40,72},{48,80},{56,88},{64,... | collective-permute-start | bytes 196616 | tf_op jit(solution)/shard_map/ppermute | solution.py:20
  189.4 25.7 %collective-permute-start.23 = (bf16[2,128,128]{2,1,0:T(8,128)(2,1)S(1)}, bf16[2,128,128]{2,1,0:T(8,128)(2,1)S(1)}, u32[]{:S(2)}, u32[]{:S(2)}) collective-permute-start(bf16[2,128,128]{2,1,0:T(8,128)(2,1)S(1)} %get-tuple-element.16), channel_id=1, source_target_pairs={{0,24},{8,32},{16,40},{24,48},{32,56},{40,64},{48,72},{56,80},{64,... | collective-permute-start | bytes 196616 | tf_op jit(solution)/shard_map/ppermute | solution.py:20
  194.8 28.4 %collective-permute-start.22 = (bf16[2,128,128]{2,1,0:T(8,128)(2,1)S(1)}, bf16[2,128,128]{2,1,0:T(8,128)(2,1)S(1)}, u32[]{:S(2)}, u32[]{:S(2)}) collective-permute-start(bf16[2,128,128]{2,1,0:T(8,128)(2,1)S(1)} %get-tuple-element.17), channel_id=1, source_target_pairs={{0,16},{8,24},{16,32},{24,40},{32,48},{40,56},{48,64},{56,72},{64,... | collective-permute-start | bytes 196616 | tf_op jit(solution)/shard_map/ppermute | solution.py:20
  205.1 29.8 %collective-permute-start.14 = (bf16[2,128,128]{2,1,0:T(8,128)(2,1)S(1)}, bf16[2,128,128]{2,1,0:T(8,128)(2,1)S(1)}, u32[]{:S(2)}, u32[]{:S(2)}) collective-permute-start(bf16[2,128,128]{2,1,0:T(8,128)(2,1)S(1)} %get-tuple-element.4), channel_id=1, source_target_pairs={{8,0},{16,8},{24,16},{32,24},{40,32},{48,40},{56,48},{64,56},{72,6... | collective-permute-start | bytes 196616 | tf_op jit(solution)/shard_map/ppermute | solution.py:20
  207.0 29.8 %collective-permute-start.20 = (bf16[2,128,128]{2,1,0:T(8,128)(2,1)S(1)}, bf16[2,128,128]{2,1,0:T(8,128)(2,1)S(1)}, u32[]{:S(2)}, u32[]{:S(2)}) collective-permute-start(bf16[2,128,128]{2,1,0:T(8,128)(2,1)S(1)} %get-tuple-element.5), channel_id=1, source_target_pairs={{56,0},{64,8},{72,16},{80,24},{88,32},{96,40},{104,48},{112,56},{1... | collective-permute-start | bytes 196616 | tf_op jit(solution)/shard_map/ppermute | solution.py:20
  209.0 31.2 %collective-permute-start.19 = (bf16[2,128,128]{2,1,0:T(8,128)(2,1)S(1)}, bf16[2,128,128]{2,1,0:T(8,128)(2,1)S(1)}, u32[]{:S(2)}, u32[]{:S(2)}) collective-permute-start(bf16[2,128,128]{2,1,0:T(8,128)(2,1)S(1)} %get-tuple-element.6), channel_id=1, source_target_pairs={{48,0},{56,8},{64,16},{72,24},{80,32},{88,40},{96,48},{104,56},{11... | collective-permute-start | bytes 196616 | tf_op jit(solution)/shard_map/ppermute | solution.py:20
  215.1 25.1 %collective-permute-start.18 = (bf16[2,128,128]{2,1,0:T(8,128)(2,1)S(1)}, bf16[2,128,128]{2,1,0:T(8,128)(2,1)S(1)}, u32[]{:S(2)}, u32[]{:S(2)}) collective-permute-start(bf16[2,128,128]{2,1,0:T(8,128)(2,1)S(1)} %get-tuple-element.7), channel_id=1, source_target_pairs={{40,0},{48,8},{56,16},{64,24},{72,32},{80,40},{88,48},{96,56},{104... | collective-permute-start | bytes 196616 | tf_op jit(solution)/shard_map/ppermute | solution.py:20
  223.3 17.0 %collective-permute-start.17 = (bf16[2,128,128]{2,1,0:T(8,128)(2,1)S(1)}, bf16[2,128,128]{2,1,0:T(8,128)(2,1)S(1)}, u32[]{:S(2)}, u32[]{:S(2)}) collective-permute-start(bf16[2,128,128]{2,1,0:T(8,128)(2,1)S(1)} %get-tuple-element.8), channel_id=1, source_target_pairs={{32,0},{40,8},{48,16},{56,24},{64,32},{72,40},{80,48},{88,56},{96,... | collective-permute-start | bytes 196616 | tf_op jit(solution)/shard_map/ppermute | solution.py:20
  234.9 14.0 %collective-permute-start.16 = (bf16[2,128,128]{2,1,0:T(8,128)(2,1)S(1)}, bf16[2,128,128]{2,1,0:T(8,128)(2,1)S(1)}, u32[]{:S(2)}, u32[]{:S(2)}) collective-permute-start(bf16[2,128,128]{2,1,0:T(8,128)(2,1)S(1)} %get-tuple-element.9), channel_id=1, source_target_pairs={{24,0},{32,8},{40,16},{48,24},{56,32},{64,40},{72,48},{80,56},{88,... | collective-permute-start | bytes 196616 | tf_op jit(solution)/shard_map/ppermute | solution.py:20
  236.8 14.9 %collective-permute-start.15 = (bf16[2,128,128]{2,1,0:T(8,128)(2,1)S(1)}, bf16[2,128,128]{2,1,0:T(8,128)(2,1)S(1)}, u32[]{:S(2)}, u32[]{:S(2)}) collective-permute-start(bf16[2,128,128]{2,1,0:T(8,128)(2,1)S(1)} %get-tuple-element.10), channel_id=1, source_target_pairs={{16,0},{24,8},{32,16},{40,24},{48,32},{56,40},{64,48},{72,56},{80,... | collective-permute-start | bytes 196616 | tf_op jit(solution)/shard_map/ppermute | solution.py:20
where the time goes:
time: 254 us; the launch traced here: 253 us
  starting transfers between devices  130 us (51%)
  waiting for transfers between devices  81.9 us (32%)
  between operations  11.8 us (5%)
  matrix products  10.9 us (4%)
  local copies, waits for them, and re-layouts  9.6 us (4%)
  other arithmetic  8.66 us (3%)
    ppermute x28, starting transfers between devices, shifted(): return lax.ppermute(block, axis, route)  130 us
    ppermute x28, waiting for transfers between devices, shifted(): return lax.ppermute(block, axis, route)  81.9 us
  transfers between devices with their start and end apart: 28, of which 11 were waited for; matrix products, arithmetic and copies ran while one was open for 5% of the time, Pallas kernels for 0%

commit v1 on v0

v1 whole, which is shorter than its diff:
```python
import functools
import math

import jax
import jax.numpy as jnp
from jax import lax
from jax.experimental import pallas as pl
from jax.experimental.pallas import tpu as pltpu
from jax.sharding import PartitionSpec as P

HD = 128
GROUP = 8
TOK = 128
RUN = 8
COLS = GROUP * TOK
WIDE = 256
MASKED = -1e30
SCALE = 1.0 / math.sqrt(HD)
EXP2_SCALE = SCALE * math.log2(math.e)
UP, DOWN = 0, 1


def dot(left, right, left_dim, right_dim):
    return lax.dot_general(
        left, right, (((left_dim,), (right_dim,)), ((), ())), preferred_element_type=jnp.float32
    )


def rows_of(slot):
    return pl.ds(pl.multiple_of(slot * TOK, TOK), TOK)


def kernel(
    runs,
    doc_ref,
    q_hbm,
    k_hbm,
    v_hbm,
    g_hbm,
    out_ref,
    qgrad_ref,
    kgrad_ref,
    vgrad_ref,
    kv,
    kv_t,
    queries,
    grads,
    scores,
    dprobs,
    peak,
    probs,
    dscores,
    acc,
    own,
    snd,
    rcv,
    rcv_y,
    local_sem,
    load_sem,
    fetch_send,
    fetch_recv,
    fetch_y_send,
    fetch_y_recv,
    back_send,
    back_recv,
    back_y_send,
    back_y_recv,
):
    index = lax.axis_index("ctx")
    run = lax.div(index, RUN)
    place = lax.rem(index, RUN)
    next_run = lax.rem(run + 1, runs) * RUN + place
    last_run = lax.rem(run + runs - 1, runs) * RUN + place
    has_below = place >= 1
    has_above = place <= RUN - 2

    def copy(src, dst, send, recv, target):
        return pltpu.make_async_remote_copy(
            src_ref=src,
            dst_ref=dst,
            send_sem=send,
            recv_sem=recv,
            device_id={"ctx": target},
            device_id_type=pl.DeviceIdType.MESH,
        )

    kv_loads = []
    for piece in range(2):
        for part, source in enumerate((k_hbm, v_hbm)):
            kv_loads.append(
                pltpu.make_async_copy(
                    source.at[piece], kv.at[piece, place, part], local_sem.at[piece, part]
                )
            )
    for load in kv_loads:
        load.start()
    loads = []
    for piece in range(2):
        for which, (source, target) in enumerate(((q_hbm, queries), (g_hbm, grads))):
            for head in range(GROUP):
                span = pl.ds(head * TOK, TOK)
                loads.append(
                    pltpu.make_async_copy(
                        source.at[piece, :, span],
                        target.at[piece, span],
                        load_sem.at[piece, which, head],
                    )
                )
    for load in loads:
        load.start()

    barrier = pltpu.get_barrier_semaphore()

    def greet(target):
        pl.semaphore_signal(
            barrier, inc=1, device_id={"ctx": target}, device_id_type=pl.DeviceIdType.MESH
        )

    greet(next_run)
    greet(last_run)

    @pl.when(has_below)
    def _():
        greet(index - 1)

    @pl.when(has_above)
    def _():
        greet(index + 1)

    peers = 2 + has_below.astype(jnp.int32) + has_above.astype(jnp.int32)
    pl.semaphore_wait(barrier, peers)

    for load in kv_loads:
        load.wait()

    def fetch_y(piece):
        return copy(
            kv.at[piece, place],
            kv.at[piece, RUN],
            fetch_y_send.at[piece],
            fetch_y_recv.at[piece],
            (next_run, last_run)[piece],
        )

    def fetch(direction, piece, step, source, slot):
        return copy(
            kv.at[piece, source],
            kv.at[piece, slot],
            fetch_send.at[direction, piece, step],
            fetch_recv.at[direction, piece, step],
            index + 1 if direction == UP else index - 1,
        )

    y_needed = (has_below, has_above)
    for piece in range(2):

        @pl.when(y_needed[piece])
        def _(piece=piece):
            fetch_y(piece).start()

    @pl.when(has_above)
    def _():
        fetch(UP, 0, 0, place, place).start()

    @pl.when(has_below)
    def _():
        fetch(DOWN, 1, 0, place, place).start()

    for load in loads:
        load.wait()

    def doc_of(piece, run_of_slot, slot):
        at = run_of_slot * RUN + slot
        inside = (at >= 0) & (at < runs * RUN)
        at = jnp.clip(at, 0, runs * RUN - 1)
        block = at if piece == 0 else 2 * runs * RUN - 1 - at
        return jnp.where(inside, doc_ref[block], -1)

    my_docs = [doc_of(piece, run, place) for piece in range(2)]
    key_row = lax.broadcasted_iota(jnp.int32, (TOK, WIDE), 0)
    query_row = lax.rem(lax.broadcasted_iota(jnp.int32, (TOK, WIDE), 1), TOK)
    causal = key_row <= query_row

    def visit(slot, is_own):
        for piece in range(2):
            keys = kv[piece, slot, 0]
            vals = kv[piece, slot, 1]
            kv_t[piece, 0, :, rows_of(slot)] = keys.T
            kv_t[piece, 1, :, rows_of(slot)] = vals.T
            if not is_own:
                if piece == 0:
                    run_of_slot = jnp.where(slot > place, run - 1, run)
                else:
                    run_of_slot = jnp.where(slot < place, run + 1, run)
                doc = doc_of(piece, run_of_slot, slot)
                bias = jnp.where(doc == my_docs[piece], 0.0, MASKED)
            for first in range(0, COLS, WIDE):
                cols = pl.ds(first, WIDE)
                block = dot(keys, queries[piece, cols], 1, 1)
                if is_own:
                    block = jnp.where(causal, block, MASKED)
                else:
                    block = block + bias
                scores[piece, rows_of(slot), cols] = block
                top = jnp.max(block.reshape(TOK // 8, 8, WIDE), axis=0)
                if not is_own:
                    top = jnp.maximum(top, peak[piece, :, cols])
                peak[piece, :, cols] = top
                dprobs[piece, rows_of(slot), cols] = dot(vals, grads[piece, cols], 1, 1)

    visit(place, True)

    @pl.when(has_above)
    def _():
        fetch_y(1).wait_recv()
        fetch(UP, 1, 0, RUN, place).start()

    @pl.when(has_below)
    def _():
        fetch_y(0).wait_recv()
        fetch(DOWN, 0, 0, RUN, place).start()

    def fetch_step(step, carry):
        below = place - 1 - step
        above = place + 1 + step

        @pl.when(below >= 0)
        def _():
            for piece in range(2):
                fetch(UP, piece, step, below, below).wait_recv()

                @pl.when(has_above)
                def _(piece=piece):
                    fetch(UP, piece, step + 1, below, below).start()

        @pl.when(above < RUN)
        def _():
            for piece in (1, 0):
                fetch(DOWN, piece, step, above, above).wait_recv()

                @pl.when(has_below)
                def _(piece=piece):
                    fetch(DOWN, piece, step + 1, above, above).start()

        @pl.when(below >= 0)
        def _():
            visit(below, False)

        @pl.when(above < RUN)
        def _():
            visit(above, False)

        return carry

    lax.fori_loop(0, RUN - 1, fetch_step, 0)

    def soften(group, carry):
        for piece in range(2):
            cols = pl.ds(pl.multiple_of(group * WIDE, WIDE), WIDE)
            top = jnp.max(peak[piece, :, cols], axis=0, keepdims=True)
            total = jnp.zeros((8, WIDE), jnp.float32)
            delta = jnp.zeros((8, WIDE), jnp.float32)
            for slot in range(RUN):
                rows = pl.ds(slot * TOK, TOK)
                weight = jnp.exp2((scores[piece, rows, cols] - top) * EXP2_SCALE)
                scores[piece, rows, cols] = weight
                total += jnp.sum(weight.reshape(TOK // 8, 8, WIDE), axis=0)
                delta += jnp.sum(
                    (weight * dprobs[piece, rows, cols]).reshape(TOK // 8, 8, WIDE), axis=0
                )
            inverse = 1.0 / jnp.sum(total, axis=0, keepdims=True)
            delta = jnp.sum(delta, axis=0, keepdims=True) * inverse
            for slot in range(RUN):
                rows = pl.ds(slot * TOK, TOK)
                prob = scores[piece, rows, cols] * inverse
                probs[piece, rows, cols] = prob.astype(jnp.bfloat16)
                dscores[piece, rows, cols] = (prob * (dprobs[piece, rows, cols] - delta)).astype(
                    jnp.bfloat16
                )
        return carry

    lax.fori_loop(0, COLS // WIDE, soften, 0)

    def key_side(piece, slot):
        rows = rows_of(slot)
        return (
            dot(dscores[piece, rows, :], queries[piece], 1, 0) * SCALE,
            dot(probs[piece, rows, :], grads[piece], 1, 0),
        )

    def back(direction, piece, step, slot):
        return copy(
            snd.at[piece, slot],
            rcv.at[direction, piece, slot],
            back_send.at[direction, piece, step],
            back_recv.at[direction, piece, step],
            index + 1 if direction == UP else index - 1,
        )

    def back_step(step, carry):
        low = step - (RUN - 1) + place
        high = RUN - 1 - step + place
        todo = (
            (DOWN, low >= 0, low, has_above),
            (UP, high < RUN, high, has_below),
        )
        for direction, active, slot, _ in todo:

            @pl.when(active)
            def _(direction=direction, slot=slot):
                for piece in range(2):
                    for part, value in enumerate(key_side(piece, slot)):
                        acc[direction, piece, part] = value

        for direction, active, slot, receives in todo:

            @pl.when(active)
            def _(direction=direction, slot=slot, receives=receives):
                for piece in range(2):

                    @pl.when(receives)
                    def _(piece=piece):
                        back(direction, piece, step - 1, slot).wait_recv()
                        acc[direction, piece] += rcv[direction, piece, slot].astype(jnp.float32)

                    snd[piece, slot] = acc[direction, piece].astype(jnp.bfloat16)
                    back(direction, piece, step, slot).start()

        return carry

    lax.fori_loop(0, RUN - 1, back_step, 0)

    def back_y(piece):
        return copy(
            rcv.at[(UP, DOWN)[piece], piece, place],
            rcv_y.at[piece],
            back_y_send.at[piece],
            back_y_recv.at[piece],
            (last_run, next_run)[piece],
        )

    for piece in range(2):
        for part, value in enumerate(key_side(piece, place)):
            own[piece, part] = value

    @pl.when(has_below)
    def _():
        for piece in range(2):
            back(UP, piece, RUN - 2, place).wait_recv()
        back_y(0).start()
        own[1] += rcv[UP, 1, place].astype(jnp.float32)

    @pl.when(has_above)
    def _():
        for piece in (1, 0):
            back(DOWN, piece, RUN - 2, place).wait_recv()
        back_y(1).start()
        own[0] += rcv[DOWN, 0, place].astype(jnp.float32)

    def query_side(group, carry):
        for piece in range(2):
            cols = pl.ds(pl.multiple_of(group * WIDE, WIDE), WIDE)
            attended = dot(kv_t[piece, 1], probs[piece, :, cols], 1, 0)
            out_ref[piece, :, cols] = jnp.concatenate(
                [attended[:, :TOK].T, attended[:, TOK:].T], axis=1
            ).astype(jnp.bfloat16)
            pulled = dot(kv_t[piece, 0], dscores[piece, :, cols], 1, 0) * SCALE
            qgrad_ref[piece, :, cols] = jnp.concatenate(
                [pulled[:, :TOK].T, pulled[:, TOK:].T], axis=1
            ).astype(jnp.bfloat16)
        return carry

    lax.fori_loop(0, COLS // WIDE, query_side, 0)

    for piece in range(2):

        @pl.when(y_needed[piece])
        def _(piece=piece):
            back_y(piece).wait_recv()
            own[piece] += rcv_y[piece].astype(jnp.float32)

        kgrad_ref[piece] = own[piece, 0].astype(jnp.bfloat16)
        vgrad_ref[piece] = own[piece, 1].astype(jnp.bfloat16)

    for piece in range(2):

        @pl.when(y_needed[piece])
        def _(piece=piece):
            fetch_y(piece).wait_send()
            back_y(piece).wait_send()

    def drain(step, carry):
        for piece in range(2):

            @pl.when(has_above & (place - step >= 0))
            def _(piece=piece):
                fetch(UP, piece, step, place, place).wait_send()

            @pl.when(has_below & (place + step < RUN))
            def _(piece=piece):
                fetch(DOWN, piece, step, place, place).wait_send()

            @pl.when(step - (RUN - 1) + place >= 0)
            def _(piece=piece):
                back(DOWN, piece, step, place).wait_send()

            @pl.when(RUN - 1 - step + place < RUN)
            def _(piece=piece):
                back(UP, piece, step, place).wait_send()

        return carry

    lax.fori_loop(0, RUN - 1, drain, 0)


def local(queries, keys, values, out_grad, block_doc):
    runs = lax.axis_size("ctx") // RUN
    bf16, f32 = jnp.bfloat16, jnp.float32
    wide = (2, TOK, COLS)
    thin = (2, TOK, HD)
    any_space = pl.BlockSpec(memory_space=pl.ANY)
    vmem = pl.BlockSpec(memory_space=pltpu.VMEM)
    dma = pltpu.SemaphoreType.DMA
    results = pl.pallas_call(
        functools.partial(kernel, runs),
        out_shape=[
            jax.ShapeDtypeStruct(wide, bf16),
            jax.ShapeDtypeStruct(wide, bf16),
            jax.ShapeDtypeStruct(thin, bf16),
            jax.ShapeDtypeStruct(thin, bf16),
        ],
        in_specs=[pl.BlockSpec(memory_space=pltpu.SMEM)] + [any_space] * 4,
        out_specs=[vmem] * 4,
        scratch_shapes=[
            pltpu.VMEM((2, RUN + 1, 2, TOK, HD), bf16),
            pltpu.VMEM((2, 2, HD, RUN * TOK), bf16),
            pltpu.VMEM((2, COLS, HD), bf16),
            pltpu.VMEM((2, COLS, HD), bf16),
            pltpu.VMEM((2, RUN * TOK, COLS), f32),
            pltpu.VMEM((2, RUN * TOK, COLS), f32),
            pltpu.VMEM((2, 8, COLS), f32),
            pltpu.VMEM((2, RUN * TOK, COLS), bf16),
            pltpu.VMEM((2, RUN * TOK, COLS), bf16),
            pltpu.VMEM((2, 2, 2, TOK, HD), f32),
            pltpu.VMEM((2, 2, TOK, HD), f32),
            pltpu.VMEM((2, RUN, 2, TOK, HD), bf16),
            pltpu.VMEM((2, 2, RUN, 2, TOK, HD), bf16),
            pltpu.VMEM((2, 2, TOK, HD), bf16),
            dma((2, 2)),
            dma((2, 2, GROUP)),
            dma((2, 2, RUN)),
            dma((2, 2, RUN)),
            dma((2,)),
            dma((2,)),
            dma((2, 2, RUN)),
            dma((2, 2, RUN)),
            dma((2,)),
            dma((2,)),
        ],
        compiler_params=pltpu.CompilerParams(
            collective_id=0, has_side_effects=True, vmem_limit_bytes=60 * 1024 * 1024
        ),
    )(
        block_doc,
        queries.reshape(wide),
        keys.reshape(thin),
        values.reshape(thin),
        out_grad.reshape(wide),
    )
    return tuple(array[:, None] for array in results)


def solution(mesh):
    spec = P(None, "ctx", None, "tp")
    return jax.shard_map(
        local,
        mesh=mesh,
        in_specs=(spec, spec, spec, spec, P()),
        out_specs=(spec, spec, spec, spec),
        check_vma=False,
    )
```

time: 254 us -> 86 us (0.34)
  the two profiles are of different devices: /device:TPU:728 before, /device:TPU:64 now
where the time goes in v1:
time: 86 us; the launch traced here: 85.7 us
  Pallas kernels  80.7 us (94%)
  local copies, waits for them, and re-layouts  4.28 us (5%)
    pallas_call x1, Pallas kernels, local(): pl.pallas_call(functools.partial(kernel, runs), out_shape=[jax.ShapeDtype...  80.7 us
    unnamed x10, local copies, waits for them, and re-layouts  4.28 us

profile of v1, /device:TPU:64, one launch (start us, length us, event | category | flops | bytes accessed | tf_op | source)
XLA Modules:
  0.0 85.7 jit_solution(7817066804078723340)
XLA Ops:
  0.6 80.7 %shard_map.84 = (bf16[2,128,1024]{2,1,0:T(8,128)(2,1)}, bf16[2,128,1024]{2,1,0:T(8,128)(2,1)}, bf16[2,128,128]{2,1,0:T(8,128)(2,1)}, bf16[2,128,128]{2,1,0:T(8,128)(2,1)}) custom-call(s32[256]{0:T(256)} %doc_ref.1, bf16[2,128,1024]{2,1,0:T(8,128)(2,1)} %bitcast.18, bf16[2,128,128]{2,1,0:T(8,128)(2,1)} %bitcast.22, bf16[2,128,128]{2,1,0:T(8,128)(2,1)} %bitcast.23, ...), custom_call_target="tpu_custom_call" | custom-call | tf_op jit(solution)/shard_map/pallas_call | solution.py:424
  81.4 0.0 copy-start
  81.4 1.9 %copy.17 = bf16[2,1,128,1024]{3,2,1,0:T(8,128)(2,1)} copy(bf16[2,1,128,1024]{3,2,1,0:T(8,128)(2,1)} %bitcast.17) | data formatting | bytes 1048576
  83.3 0.0 copy-done
  83.3 0.0 copy-start.2
  83.3 0.8 copy.18
  84.1 0.1 copy-done.2
  84.2 0.0 copy-start.1
  84.2 0.6 copy.19
  84.8 0.2 copy-done.1
  85.0 0.6 copy.20
Async XLA Ops:
  81.4 1.9 %copy-start = (bf16[2,128,1024]{2,1,0:T(8,128)(2,1)S(1)}, bf16[2,128,1024]{2,1,0:T(8,128)(2,1)}, u32[]{:S(2)}) copy-start(bf16[2,128,1024]{2,1,0:T(8,128)(2,1)} %get-tuple-element.9) | copy-start | bytes 1572868
  83.3 0.9 %copy-start.2 = (bf16[2,128,128]{2,1,0:T(8,128)(2,1)S(1)}, bf16[2,128,128]{2,1,0:T(8,128)(2,1)}, u32[]{:S(2)}) copy-start(bf16[2,128,128]{2,1,0:T(8,128)(2,1)} %get-tuple-element.10) | copy-start | bytes 196612
  84.2 0.9 %copy-start.1 = (bf16[2,128,128]{2,1,0:T(8,128)(2,1)S(1)}, bf16[2,128,128]{2,1,0:T(8,128)(2,1)}, u32[]{:S(2)}) copy-start(bf16[2,128,128]{2,1,0:T(8,128)(2,1)} %get-tuple-element.11) | copy-start | bytes 196612

commit v2 on v1

v2 whole, which is shorter than its diff:
```python
import functools
import math

import jax
import jax.numpy as jnp
from jax import lax
from jax.experimental import pallas as pl
from jax.experimental.pallas import tpu as pltpu
from jax.sharding import PartitionSpec as P

HD = 128
GROUP = 8
TOK = 128
RUN = 8
COLS = GROUP * TOK
WIDE = 256
MASKED = -1e30
SCALE = 1.0 / math.sqrt(HD)
EXP2_SCALE = SCALE * math.log2(math.e)
UP, DOWN = 0, 1
VMEM_LIMIT = 44 * 1024 * 1024


def dot(left, right, left_dim, right_dim):
    return lax.dot_general(
        left, right, (((left_dim,), (right_dim,)), ((), ())), preferred_element_type=jnp.float32
    )


def rows_of(slot):
    return pl.ds(pl.multiple_of(slot * TOK, TOK), TOK)


def kernel(
    runs,
    doc_ref,
    q_hbm,
    k_hbm,
    v_hbm,
    g_hbm,
    out_ref,
    qgrad_ref,
    kgrad_ref,
    vgrad_ref,
    kv,
    kv_t,
    queries,
    grads,
    scores,
    dprobs,
    peak,
    probs,
    dscores,
    acc,
    own,
    snd,
    rcv,
    local_sem,
    load_sem,
    fetch_send,
    fetch_recv,
    back_send,
    back_recv,
):
    index = lax.axis_index("ctx")
    run = lax.div(index, RUN)
    place = lax.rem(index, RUN)
    after = lax.rem(run + 1, runs)
    before = lax.rem(run + runs - 1, runs)
    ahead = (1, -1)
    room = (RUN - 1 - place, place)
    trees = ((UP, 0), (DOWN, 1), (UP, 1), (DOWN, 0))
    receivers_run = {(UP, 0): run, (UP, 1): before, (DOWN, 0): after, (DOWN, 1): run}
    owners_run = {(UP, 0): run, (UP, 1): after, (DOWN, 0): before, (DOWN, 1): run}

    def copy(src, dst, send, recv, target):
        return pltpu.make_async_remote_copy(
            src_ref=src,
            dst_ref=dst,
            send_sem=send,
            recv_sem=recv,
            device_id={"ctx": target},
            device_id_type=pl.DeviceIdType.MESH,
        )

    kv_loads = []
    for piece in range(2):
        for part, source in enumerate((k_hbm, v_hbm)):
            kv_loads.append(
                pltpu.make_async_copy(
                    source.at[piece], kv.at[piece, place, part], local_sem.at[piece, part]
                )
            )
    for load in kv_loads:
        load.start()
    loads = []
    for piece in range(2):
        for which, (source, target) in enumerate(((q_hbm, queries), (g_hbm, grads))):
            for head in range(GROUP):
                span = pl.ds(head * TOK, TOK)
                loads.append(
                    pltpu.make_async_copy(
                        source.at[piece, :, span],
                        target.at[piece, span],
                        load_sem.at[piece, which, head],
                    )
                )
    for load in loads:
        load.start()

    barrier = pltpu.get_barrier_semaphore()

    for direction in (UP, DOWN):
        for away in (1, 2):

            @pl.when(room[direction] >= away)
            def _(direction=direction, away=away):
                for at_run in (run, receivers_run[direction, 1 - direction]):
                    pl.semaphore_signal(
                        barrier,
                        inc=1,
                        device_id={"ctx": at_run * RUN + place + ahead[direction] * away},
                        device_id_type=pl.DeviceIdType.MESH,
                    )

    peers = 2 * (jnp.minimum(room[UP], 2) + jnp.minimum(room[DOWN], 2))
    pl.semaphore_wait(barrier, peers)

    for load in kv_loads:
        load.wait()

    def fetch(direction, piece, part, distance, slot, at_run, away):
        return copy(
            kv.at[piece, slot, part],
            kv.at[piece, slot, part],
            fetch_send.at[direction, piece, part, distance],
            fetch_recv.at[direction, piece, part, distance],
            at_run * RUN + place + ahead[direction] * away,
        )

    for away in (2, 1):
        for part in range(2):
            for direction, piece in trees:

                @pl.when(room[direction] >= away)
                def _(direction=direction, piece=piece, part=part, away=away):
                    at_run = receivers_run[direction, piece]
                    fetch(direction, piece, part, away, place, at_run, away).start()

    def doc_of(piece, run_of_slot, slot):
        at = run_of_slot * RUN + slot
        inside = (at >= 0) & (at < runs * RUN)
        at = jnp.clip(at, 0, runs * RUN - 1)
        block = at if piece == 0 else 2 * runs * RUN - 1 - at
        return jnp.where(inside, doc_ref[block], -1)

    my_docs = [doc_of(piece, run, place) for piece in range(2)]
    key_row = lax.broadcasted_iota(jnp.int32, (TOK, WIDE), 0)
    query_row = lax.rem(lax.broadcasted_iota(jnp.int32, (TOK, WIDE), 1), TOK)
    causal = key_row <= query_row

    def visit(slot, is_own):
        for piece in range(2):
            keys = kv[piece, slot, 0]
            vals = kv[piece, slot, 1]
            kv_t[piece, 0, :, rows_of(slot)] = keys.T
            kv_t[piece, 1, :, rows_of(slot)] = vals.T
            if not is_own:
                if piece == 0:
                    run_of_slot = jnp.where(slot > place, run - 1, run)
                else:
                    run_of_slot = jnp.where(slot < place, run + 1, run)
                doc = doc_of(piece, run_of_slot, slot)
                bias = jnp.where(doc == my_docs[piece], 0.0, MASKED)
            for first in range(0, COLS, WIDE):
                cols = pl.ds(first, WIDE)
                block = dot(keys, queries[piece, cols], 1, 1)
                if is_own:
                    block = jnp.where(causal, block, MASKED)
                else:
                    block = block + bias
                scores[piece, rows_of(slot), cols] = block
                top = jnp.max(block.reshape(TOK // 8, 8, WIDE), axis=0)
                if not is_own:
                    top = jnp.maximum(top, peak[piece, :, cols])
                peak[piece, :, cols] = top
                dprobs[piece, rows_of(slot), cols] = dot(vals, grads[piece, cols], 1, 1)

    for load in loads:
        load.wait()
    visit(place, True)

    def slot_at(direction, distance):
        return place - ahead[direction] * distance, room[1 - direction] >= distance

    def fetch_step(step, carry):
        for part in range(2):
            for direction, piece in trees:
                distance = 2 * step + 2
                slot, present = slot_at(direction, distance)

                @pl.when(present)
                def _(direction=direction, piece=piece, part=part, slot=slot, distance=distance):
                    fetch(direction, piece, part, distance, slot, run, 1).wait_recv()
                    for away in (2, 1):

                        @pl.when(room[direction] >= away)
                        def _(away=away):
                            fetch(
                                direction, piece, part, distance + away, slot, run, away
                            ).start()

        for part in range(2):
            for direction, piece in trees:
                distance = 2 * step + 1
                slot, present = slot_at(direction, distance)

                @pl.when(present)
                def _(direction=direction, piece=piece, part=part, slot=slot, distance=distance):
                    fetch(direction, piece, part, distance, slot, run, 1).wait_recv()

        def visit_pair(which, carry):
            for direction in (UP, DOWN):
                slot, present = slot_at(direction, 2 * step + 1 + which)

                @pl.when(present)
                def _(slot=slot):
                    visit(slot, False)

            return carry

        return lax.fori_loop(0, 2, visit_pair, carry)

    lax.fori_loop(0, RUN // 2, fetch_step, 0)

    def soften(group, carry):
        for piece in range(2):
            cols = pl.ds(pl.multiple_of(group * WIDE, WIDE), WIDE)
            top = jnp.max(peak[piece, :, cols], axis=0, keepdims=True)
            total = jnp.zeros((8, WIDE), jnp.float32)
            delta = jnp.zeros((8, WIDE), jnp.float32)
            for slot in range(RUN):
                rows = pl.ds(slot * TOK, TOK)
                weight = jnp.exp2((scores[piece, rows, cols] - top) * EXP2_SCALE)
                scores[piece, rows, cols] = weight
                total += jnp.sum(weight.reshape(TOK // 8, 8, WIDE), axis=0)
                delta += jnp.sum(
                    (weight * dprobs[piece, rows, cols]).reshape(TOK // 8, 8, WIDE), axis=0
                )
            inverse = 1.0 / jnp.sum(total, axis=0, keepdims=True)
            delta = jnp.sum(delta, axis=0, keepdims=True) * inverse
            for slot in range(RUN):
                rows = pl.ds(slot * TOK, TOK)
                prob = scores[piece, rows, cols] * inverse
                probs[piece, rows, cols] = prob.astype(jnp.bfloat16)
                dscores[piece, rows, cols] = (prob * (dprobs[piece, rows, cols] - delta)).astype(
                    jnp.bfloat16
                )
        return carry

    lax.fori_loop(0, COLS // WIDE, soften, 0)

    def key_side(piece, slot):
        rows = rows_of(slot)
        return (
            dot(dscores[piece, rows, :], queries[piece], 1, 0) * SCALE,
            dot(probs[piece, rows, :], grads[piece], 1, 0),
        )

    def back(direction, piece, part, distance, slot, even, owner_is_next):
        at_run = jnp.where(owner_is_next, owners_run[direction, piece], run)
        return copy(
            snd.at[piece, slot, part],
            rcv.at[direction, piece, even, slot, part],
            back_send.at[direction, piece, part, distance],
            back_recv.at[direction, piece, part, distance],
            at_run * RUN + place - ahead[direction] * (1 + even),
        )

    def odd_step(step, carry):
        distance = RUN - 1 - 2 * step
        for direction, piece in trees:
            slot, present = slot_at(direction, distance)

            @pl.when(present)
            def _(direction=direction, piece=piece, slot=slot):
                for part, value in enumerate(key_side(piece, slot)):
                    snd[piece, slot, part] = value.astype(jnp.bfloat16)
                    back(direction, piece, part, distance, slot, 0, distance == 1).start()

        return carry

    lax.fori_loop(0, RUN // 2, odd_step, 0)

    def gather(total, direction, piece, part, distance, slot):
        for even in (0, 1):

            @pl.when(room[direction] > even)
            def _(even=even):
                child = distance + 1 + even
                back(direction, piece, part, child, slot, even, False).wait_recv()
                total[...] += rcv[direction, piece, even, slot, part].astype(jnp.float32)

    def even_step(step, carry):
        distance = RUN - 2 - 2 * step
        for direction, piece in trees:
            slot, present = slot_at(direction, distance)

            @pl.when(present)
            def _(direction=direction, piece=piece, slot=slot):
                for part, value in enumerate(key_side(piece, slot)):
                    acc[direction, piece, part] = value

        for part in range(2):
            for direction, piece in trees:
                slot, present = slot_at(direction, distance)

                @pl.when(present)
                def _(direction=direction, piece=piece, part=part, slot=slot):
                    total = acc.at[direction, piece, part]
                    gather(total, direction, piece, part, distance, slot)
                    snd[piece, slot, part] = total[...].astype(jnp.bfloat16)
                    back(direction, piece, part, distance, slot, 1, distance == 2).start()

        return carry

    lax.fori_loop(0, RUN // 2 - 1, even_step, 0)

    for piece in range(2):
        for part, value in enumerate(key_side(piece, place)):
            own[piece, part] = value

    def query_side(group, carry):
        for piece in range(2):
            cols = pl.ds(pl.multiple_of(group * WIDE, WIDE), WIDE)
            attended = dot(kv_t[piece, 1], probs[piece, :, cols], 1, 0)
            out_ref[piece, :, cols] = jnp.concatenate(
                [attended[:, :TOK].T, attended[:, TOK:].T], axis=1
            ).astype(jnp.bfloat16)
            pulled = dot(kv_t[piece, 0], dscores[piece, :, cols], 1, 0) * SCALE
            qgrad_ref[piece, :, cols] = jnp.concatenate(
                [pulled[:, :TOK].T, pulled[:, TOK:].T], axis=1
            ).astype(jnp.bfloat16)
        return carry

    lax.fori_loop(0, COLS // WIDE, query_side, 0)

    for part in range(2):
        for direction, piece in trees:
            gather(own.at[piece, part], direction, piece, part, 0, place)

    for piece in range(2):
        kgrad_ref[piece] = own[piece, 0].astype(jnp.bfloat16)
        vgrad_ref[piece] = own[piece, 1].astype(jnp.bfloat16)

    def drain(step, carry):
        distance = step + 1
        away = 1 + lax.rem(step, 2)
        for direction, piece in trees:
            for part in range(2):

                @pl.when((room[1 - direction] >= distance - away) & (room[direction] >= away))
                def _(direction=direction, piece=piece, part=part):
                    fetch(direction, piece, part, distance, place, run, 1).wait_send()

                @pl.when(room[1 - direction] >= distance)
                def _(direction=direction, piece=piece, part=part):
                    back(direction, piece, part, distance, place, 0, False).wait_send()

        return carry

    lax.fori_loop(0, RUN - 1, drain, 0)


def local(queries, keys, values, out_grad, block_doc):
    runs = lax.axis_size("ctx") // RUN
    bf16, f32 = jnp.bfloat16, jnp.float32
    wide = (2, TOK, COLS)
    thin = (2, TOK, HD)
    any_space = pl.BlockSpec(memory_space=pltpu.HBM)
    vmem = pl.BlockSpec(memory_space=pltpu.VMEM)
    dma = pltpu.SemaphoreType.DMA
    results = pl.pallas_call(
        functools.partial(kernel, runs),
        out_shape=[
            jax.ShapeDtypeStruct(wide, bf16),
            jax.ShapeDtypeStruct(wide, bf16),
            jax.ShapeDtypeStruct(thin, bf16),
            jax.ShapeDtypeStruct(thin, bf16),
        ],
        in_specs=[pl.BlockSpec(memory_space=pltpu.SMEM)] + [any_space] * 4,
        out_specs=[vmem] * 4,
        scratch_shapes=[
            pltpu.VMEM((2, RUN, 2, TOK, HD), bf16),
            pltpu.VMEM((2, 2, HD, RUN * TOK), bf16),
            pltpu.VMEM((2, COLS, HD), bf16),
            pltpu.VMEM((2, COLS, HD), bf16),
            pltpu.VMEM((2, RUN * TOK, COLS), f32),
            pltpu.VMEM((2, RUN * TOK, COLS), f32),
            pltpu.VMEM((2, 8, COLS), f32),
            pltpu.VMEM((2, RUN * TOK, COLS), bf16),
            pltpu.VMEM((2, RUN * TOK, COLS), bf16),
            pltpu.VMEM((2, 2, 2, TOK, HD), f32),
            pltpu.VMEM((2, 2, TOK, HD), f32),
            pltpu.VMEM((2, RUN, 2, TOK, HD), bf16),
            pltpu.VMEM((2, 2, 2, RUN, 2, TOK, HD), bf16),
            dma((2, 2)),
            dma((2, 2, GROUP)),
            dma((2, 2, 2, RUN)),
            dma((2, 2, 2, RUN)),
            dma((2, 2, 2, RUN)),
            dma((2, 2, 2, RUN)),
        ],
        compiler_params=pltpu.CompilerParams(
            collective_id=0, has_side_effects=True, vmem_limit_bytes=VMEM_LIMIT
        ),
    )(
        block_doc,
        queries.reshape(wide),
        keys.reshape(thin),
        values.reshape(thin),
        out_grad.reshape(wide),
    )
    return tuple(array[:, None] for array in results)


def solution(mesh):
    spec = P(None, "ctx", None, "tp")
    return jax.shard_map(
        local,
        mesh=mesh,
        in_specs=(spec, spec, spec, spec, P()),
        out_specs=(spec, spec, spec, spec),
        check_vma=False,
    )
```

time: 86 us -> 87.5 us (1.017)
  the two profiles are of different devices: /device:TPU:64 before, /device:TPU:256 now
where the time goes in v2:
time: 87.5 us; the launch traced here: 87.1 us
  Pallas kernels  79.2 us (91%)
  local copies, waits for them, and re-layouts  7.28 us (8%)
    pallas_call x1, Pallas kernels, local(): pl.pallas_call(functools.partial(kernel, runs), out_shape=[jax.ShapeDtype...  79.2 us
    unnamed x14, local copies, waits for them, and re-layouts  7.28 us

profile of v2, /device:TPU:256, one launch (start us, length us, event | category | flops | bytes accessed | tf_op | source)
XLA Modules:
  0.0 87.1 jit_solution(3441919261464740512)
XLA Ops:
  0.6 0.0 copy-start.4
  0.6 0.7 copy-done.4
  1.3 0.0 copy-start
  1.3 1.0 %copy-done = bf16[2,1,128,1024]{3,2,1,0:T(8,128)(2,1)S(1)} copy-done((bf16[2,1,128,1024]{3,2,1,0:T(8,128)(2,1)S(1)}, bf16[2,1,128,1024]{3,2,1,0:T(8,128)(2,1)}, u32[]{:S(2)}) %copy-start) | copy-done | bytes 524312
  2.4 0.0 copy-start.1
  2.4 1.0 %copy-done.1 = bf16[2,1,128,1024]{3,2,1,0:T(8,128)(2,1)S(1)} copy-done((bf16[2,1,128,1024]{3,2,1,0:T(8,128)(2,1)S(1)}, bf16[2,1,128,1024]{3,2,1,0:T(8,128)(2,1)}, u32[]{:S(2)}) %copy-start.1) | copy-done | bytes 524312
  3.4 0.0 copy-start.2
  3.4 0.8 copy-done.2
  4.2 0.0 copy-start.3
  4.2 0.8 copy-done.3
  5.1 79.2 %shard_map.84 = (bf16[2,128,1024]{2,1,0:T(8,128)(2,1)S(1)}, bf16[2,128,1024]{2,1,0:T(8,128)(2,1)S(1)}, bf16[2,128,128]{2,1,0:T(8,128)(2,1)S(1)}, bf16[2,128,128]{2,1,0:T(8,128)(2,1)S(1)}) custom-call(s32[256]{0:T(256)S(1)} %copy-done.4, bf16[2,128,1024]{2,1,0:T(8,128)(2,1)S(1)} %bitcast.18, bf16[2,128,128]{2,1,0:T(8,128)(2,1)S(1)} %bitcast.22, ...), custom_call_target="tpu_custom_call" | custom-call | tf_op jit(solution)/shard_map/pallas_call | solution.py:383
  84.3 0.8 copy.17
  85.1 0.8 copy.18
  85.9 0.6 copy.19
  86.5 0.6 copy.20
Async XLA Ops:
  0.6 0.7 copy-start.4
  1.3 1.0 %copy-start = (bf16[2,1,128,1024]{3,2,1,0:T(8,128)(2,1)S(1)}, bf16[2,1,128,1024]{3,2,1,0:T(8,128)(2,1)}, u32[]{:S(2)}) copy-start(bf16[2,1,128,1024]{3,2,1,0:T(8,128)(2,1)} %param.5) | copy-start | bytes 1572868
  2.4 1.0 %copy-start.1 = (bf16[2,1,128,1024]{3,2,1,0:T(8,128)(2,1)S(1)}, bf16[2,1,128,1024]{3,2,1,0:T(8,128)(2,1)}, u32[]{:S(2)}) copy-start(bf16[2,1,128,1024]{3,2,1,0:T(8,128)(2,1)} %param.8) | copy-start | bytes 1572868
  3.4 0.8 copy-start.2
  4.2 0.8 copy-start.3

commit v3 on v2

--- a/solution.py
+++ b/solution.py
@@ -18,6 +18,7 @@
 SCALE = 1.0 / math.sqrt(HD)
 EXP2_SCALE = SCALE * math.log2(math.e)
 UP, DOWN = 0, 1
+LAG = 2
 VMEM_LIMIT = 44 * 1024 * 1024
 
 
@@ -138,14 +139,17 @@
             at_run * RUN + place + ahead[direction] * away,
         )
 
-    for away in (2, 1):
-        for part in range(2):
-            for direction, piece in trees:
-
-                @pl.when(room[direction] >= away)
-                def _(direction=direction, piece=piece, part=part, away=away):
-                    at_run = receivers_run[direction, piece]
-                    fetch(direction, piece, part, away, place, at_run, away).start()
+    def send_own(piece):
+        for away in (2, 1):
+            for part in range(2):
+                for direction in (UP, DOWN):
+
+                    @pl.when(room[direction] >= away)
+                    def _(direction=direction, part=part, away=away):
+                        at_run = receivers_run[direction, piece]
+                        fetch(direction, piece, part, away, place, at_run, away).start()
+
+    send_own(0)
 
     def doc_of(piece, run_of_slot, slot):
         at = run_of_slot * RUN + slot
@@ -159,65 +163,59 @@
     query_row = lax.rem(lax.broadcasted_iota(jnp.int32, (TOK, WIDE), 1), TOK)
     causal = key_row <= query_row
 
-    def visit(slot, is_own):
-        for piece in range(2):
-            keys = kv[piece, slot, 0]
-            vals = kv[piece, slot, 1]
-            kv_t[piece, 0, :, rows_of(slot)] = keys.T
-            kv_t[piece, 1, :, rows_of(slot)] = vals.T
+    def visit(piece, slot, is_own):
+        keys = kv[piece, slot, 0]
+        vals = kv[piece, slot, 1]
+        kv_t[piece, 0, :, rows_of(slot)] = keys.T
+        kv_t[piece, 1, :, rows_of(slot)] = vals.T
+        if not is_own:
+            if piece == 0:
+                run_of_slot = jnp.where(slot > place, run - 1, run)
+            else:
+                run_of_slot = jnp.where(slot < place, run + 1, run)
+            doc = doc_of(piece, run_of_slot, slot)
+            bias = jnp.where(doc == my_docs[piece], 0.0, MASKED)
+        for first in range(0, COLS, WIDE):
+            cols = pl.ds(first, WIDE)
+            block = dot(keys, queries[piece, cols], 1, 1)
+            if is_own:
+                block = jnp.where(causal, block, MASKED)
+            else:
+                block = block + bias
+            scores[piece, rows_of(slot), cols] = block
+            top = jnp.max(block.reshape(TOK // 8, 8, WIDE), axis=0)
             if not is_own:
-                if piece == 0:
-                    run_of_slot = jnp.where(slot > place, run - 1, run)
-                else:
-                    run_of_slot = jnp.where(slot < place, run + 1, run)
-                doc = doc_of(piece, run_of_slot, slot)
-                bias = jnp.where(doc == my_docs[piece], 0.0, MASKED)
-            for first in range(0, COLS, WIDE):
-                cols = pl.ds(first, WIDE)
-                block = dot(keys, queries[piece, cols], 1, 1)
-                if is_own:
-                    block = jnp.where(causal, block, MASKED)
-                else:
-                    block = block + bias
-                scores[piece, rows_of(slot), cols] = block
-                top = jnp.max(block.reshape(TOK // 8, 8, WIDE), axis=0)
-                if not is_own:
-                    top = jnp.maximum(top, peak[piece, :, cols])
-                peak[piece, :, cols] = top
-                dprobs[piece, rows_of(slot), cols] = dot(vals, grads[piece, cols], 1, 1)
+                top = jnp.maximum(top, peak[piece, :, cols])
+            peak[piece, :, cols] = top
+            dprobs[piece, rows_of(slot), cols] = dot(vals, grads[piece, cols], 1, 1)
 
     for load in loads:
         load.wait()
-    visit(place, True)
+    for piece in range(2):
+        visit(piece, place, True)
 
     def slot_at(direction, distance):
         return place - ahead[direction] * distance, room[1 - direction] >= distance
 
-    def fetch_step(step, carry):
-        for part in range(2):
-            for direction, piece in trees:
-                distance = 2 * step + 2
-                slot, present = slot_at(direction, distance)
-
-                @pl.when(present)
-                def _(direction=direction, piece=piece, part=part, slot=slot, distance=distance):
-                    fetch(direction, piece, part, distance, slot, run, 1).wait_recv()
-                    for away in (2, 1):
-
-                        @pl.when(room[direction] >= away)
-                        def _(away=away):
-                            fetch(
-                                direction, piece, part, distance + away, slot, run, away
-                            ).start()
-
-        for part in range(2):
-            for direction, piece in trees:
-                distance = 2 * step + 1
-                slot, present = slot_at(direction, distance)
-
-                @pl.when(present)
-                def _(direction=direction, piece=piece, part=part, slot=slot, distance=distance):
-                    fetch(direction, piece, part, distance, slot, run, 1).wait_recv()
+    def fetch_step(piece, step):
+        for even in (1, 0):
+            distance = 2 * step + 1 + even
+            for part in range(2):
+                for direction in (UP, DOWN):
+                    slot, present = slot_at(direction, distance)
+
+                    @pl.when(present)
+                    def _(direction=direction, part=part, slot=slot, distance=distance, even=even):
+                        fetch(direction, piece, part, distance, slot, run, 1).wait_recv()
+                        if not even:
+                            return
+                        for away in (2, 1):
+
+                            @pl.when(room[direction] >= away)
+                            def _(away=away):
+                                fetch(
+                                    direction, piece, part, distance + away, slot, run, away
+                                ).start()
 
         def visit_pair(which, carry):
             for direction in (UP, DOWN):
@@ -225,40 +223,34 @@
 
                 @pl.when(present)
                 def _(slot=slot):
-                    visit(slot, False)
+                    visit(piece, slot, False)
 
             return carry
 
-        return lax.fori_loop(0, 2, visit_pair, carry)
-
-    lax.fori_loop(0, RUN // 2, fetch_step, 0)
-
-    def soften(group, carry):
-        for piece in range(2):
-            cols = pl.ds(pl.multiple_of(group * WIDE, WIDE), WIDE)
-            top = jnp.max(peak[piece, :, cols], axis=0, keepdims=True)
-            total = jnp.zeros((8, WIDE), jnp.float32)
-            delta = jnp.zeros((8, WIDE), jnp.float32)
-            for slot in range(RUN):
-                rows = pl.ds(slot * TOK, TOK)
-                weight = jnp.exp2((scores[piece, rows, cols] - top) * EXP2_SCALE)
-                scores[piece, rows, cols] = weight
-                total += jnp.sum(weight.reshape(TOK // 8, 8, WIDE), axis=0)
-                delta += jnp.sum(
-                    (weight * dprobs[piece, rows, cols]).reshape(TOK // 8, 8, WIDE), axis=0
-                )
-            inverse = 1.0 / jnp.sum(total, axis=0, keepdims=True)
-            delta = jnp.sum(delta, axis=0, keepdims=True) * inverse
-            for slot in range(RUN):
-                rows = pl.ds(slot * TOK, TOK)
-                prob = scores[piece, rows, cols] * inverse
-                probs[piece, rows, cols] = prob.astype(jnp.bfloat16)
-                dscores[piece, rows, cols] = (prob * (dprobs[piece, rows, cols] - delta)).astype(
-                    jnp.bfloat16
-                )
-        return carry
-
-    lax.fori_loop(0, COLS // WIDE, soften, 0)
+        lax.fori_loop(0, 2, visit_pair, 0)
+
+    def soften(piece, group):
+        cols = pl.ds(pl.multiple_of(group * WIDE, WIDE), WIDE)
+        top = jnp.max(peak[piece, :, cols], axis=0, keepdims=True)
+        total = jnp.zeros((8, WIDE), jnp.float32)
+        delta = jnp.zeros((8, WIDE), jnp.float32)
+        for slot in range(RUN):
+            rows = pl.ds(slot * TOK, TOK)
+            weight = jnp.exp2((scores[piece, rows, cols] - top) * EXP2_SCALE)
+            scores[piece, rows, cols] = weight
+            total += jnp.sum(weight.reshape(TOK // 8, 8, WIDE), axis=0)
+            delta += jnp.sum(
+                (weight * dprobs[piece, rows, cols]).reshape(TOK // 8, 8, WIDE), axis=0
+            )
+        inverse = 1.0 / jnp.sum(total, axis=0, keepdims=True)
+        delta = jnp.sum(delta, axis=0, keepdims=True) * inverse
+        for slot in range(RUN):
+            rows = pl.ds(slot * TOK, TOK)
+            prob = scores[piece, rows, cols] * inverse
+            probs[piece, rows, cols] = prob.astype(jnp.bfloat16)
+            dscores[piece, rows, cols] = (prob * (dprobs[piece, rows, cols] - delta)).astype(
+                jnp.bfloat16
+            )
 
     def key_side(piece, slot):
         rows = rows_of(slot)
@@ -277,20 +269,16 @@
             at_run * RUN + place - ahead[direction] * (1 + even),
         )
 
-    def odd_step(step, carry):
+    def odd_step(piece, step):
         distance = RUN - 1 - 2 * step
-        for direction, piece in trees:
+        for direction in (UP, DOWN):
             slot, present = slot_at(direction, distance)
 
             @pl.when(present)
-            def _(direction=direction, piece=piece, slot=slot):
+            def _(direction=direction, slot=slot):
                 for part, value in enumerate(key_side(piece, slot)):
                     snd[piece, slot, part] = value.astype(jnp.bfloat16)
                     back(direction, piece, part, distance, slot, 0, distance == 1).start()
-
-        return carry
-
-    lax.fori_loop(0, RUN // 2, odd_step, 0)
 
     def gather(total, direction, piece, part, distance, slot):
         for even in (0, 1):
@@ -301,57 +289,84 @@
                 back(direction, piece, part, child, slot, even, False).wait_recv()
                 total[...] += rcv[direction, piece, even, slot, part].astype(jnp.float32)
 
-    def even_step(step, carry):
+    def even_step(piece, step):
         distance = RUN - 2 - 2 * step
-        for direction, piece in trees:
+        for direction in (UP, DOWN):
             slot, present = slot_at(direction, distance)
 
             @pl.when(present)
-            def _(direction=direction, piece=piece, slot=slot):
+            def _(direction=direction, slot=slot):
                 for part, value in enumerate(key_side(piece, slot)):
                     acc[direction, piece, part] = value
 
         for part in range(2):
-            for direction, piece in trees:
+            for direction in (UP, DOWN):
                 slot, present = slot_at(direction, distance)
 
                 @pl.when(present)
-                def _(direction=direction, piece=piece, part=part, slot=slot):
+                def _(direction=direction, part=part, slot=slot):
                     total = acc.at[direction, piece, part]
                     gather(total, direction, piece, part, distance, slot)
                     snd[piece, slot, part] = total[...].astype(jnp.bfloat16)
                     back(direction, piece, part, distance, slot, 1, distance == 2).start()
 
-        return carry
-
-    lax.fori_loop(0, RUN // 2 - 1, even_step, 0)
-
-    for piece in range(2):
+    def query_side(piece, group):
+        cols = pl.ds(pl.multiple_of(group * WIDE, WIDE), WIDE)
+        attended = dot(kv_t[piece, 1], probs[piece, :, cols], 1, 0)
+        out_ref[piece, :, cols] = jnp.concatenate(
+            [attended[:, :TOK].T, attended[:, TOK:].T], axis=1
+        ).astype(jnp.bfloat16)
+        pulled = dot(kv_t[piece, 0], dscores[piece, :, cols], 1, 0) * SCALE
+        qgrad_ref[piece, :, cols] = jnp.concatenate(
+            [pulled[:, :TOK].T, pulled[:, TOK:].T], axis=1
+        ).astype(jnp.bfloat16)
+
+    def finish(piece):
         for part, value in enumerate(key_side(piece, place)):
             own[piece, part] = value
-
-    def query_side(group, carry):
-        for piece in range(2):
-            cols = pl.ds(pl.multiple_of(group * WIDE, WIDE), WIDE)
-            attended = dot(kv_t[piece, 1], probs[piece, :, cols], 1, 0)
-            out_ref[piece, :, cols] = jnp.concatenate(
-                [attended[:, :TOK].T, attended[:, TOK:].T], axis=1
-            ).astype(jnp.bfloat16)
-            pulled = dot(kv_t[piece, 0], dscores[piece, :, cols], 1, 0) * SCALE
-            qgrad_ref[piece, :, cols] = jnp.concatenate(
-                [pulled[:, :TOK].T, pulled[:, TOK:].T], axis=1
-            ).astype(jnp.bfloat16)
-        return carry
-
-    lax.fori_loop(0, COLS // WIDE, query_side, 0)
-
-    for part in range(2):
-        for direction, piece in trees:
-            gather(own.at[piece, part], direction, piece, part, 0, place)
-
-    for piece in range(2):
+        repeat(COLS // WIDE, query_side, piece)
+        for part in range(2):
+            for direction in (UP, DOWN):
+                gather(own.at[piece, part], direction, piece, part, 0, place)
         kgrad_ref[piece] = own[piece, 0].astype(jnp.bfloat16)
         vgrad_ref[piece] = own[piece, 1].astype(jnp.bfloat16)
+
+    def repeat(count, action, piece):
+        def body(step, carry):
+            action(piece, step)
+            return carry
+
+        lax.fori_loop(0, count, body, 0)
+
+    def stage(time, carry):
+        for piece in range(2):
+            now = time - LAG * piece
+            if piece == 1:
+
+                @pl.when(now == -1)
+                def _():
+                    send_own(1)
+
+            @pl.when((now >= 0) & (now < RUN // 2))
+            def _(piece=piece, now=now):
+                fetch_step(piece, now)
+
+            @pl.when(now == RUN // 2 - 1)
+            def _(piece=piece):
+                repeat(COLS // WIDE, soften, piece)
+                repeat(RUN // 2, odd_step, piece)
+
+            @pl.when((now >= RUN // 2) & (now < RUN - 1))
+            def _(piece=piece, now=now):
+                even_step(piece, now - RUN // 2)
+
+            @pl.when(now == RUN - 1)
+            def _(piece=piece):
+                finish(piece)
+
+        return carry
+
+    lax.fori_loop(0, RUN + LAG, stage, 0)
 
     def drain(step, carry):
         distance = step + 1

time: 87.5 us -> 85.1 us (0.973)
  Pallas kernels: 79.2 us -> 76.8 us
    pallas_call x1, Pallas kernels: 79.2 us -> 76.8 us  [local(): pl.pallas_call(functools.partial(kernel, runs), out_shape=[jax.ShapeDtype...]
where the time goes in v3:
time: 85.1 us; the launch traced here: 84.7 us
  Pallas kernels  76.8 us (90%)
  local copies, waits for them, and re-layouts  7.28 us (9%)
    pallas_call x1, Pallas kernels, local(): pl.pallas_call(functools.partial(kernel, runs), out_shape=[jax.ShapeDtype...  76.8 us
    unnamed x14, local copies, waits for them, and re-layouts  7.28 us

profile of v3, /device:TPU:256, one launch (start us, length us, event | category | flops | bytes accessed | tf_op | source)
XLA Modules:
  0.0 84.7 jit_solution(10076737645093952464)
XLA Ops:
  0.6 0.0 copy-start.4
  0.6 0.7 copy-done.4
  1.3 0.0 copy-start
  1.3 1.0 %copy-done = bf16[2,1,128,1024]{3,2,1,0:T(8,128)(2,1)S(1)} copy-done((bf16[2,1,128,1024]{3,2,1,0:T(8,128)(2,1)S(1)}, bf16[2,1,128,1024]{3,2,1,0:T(8,128)(2,1)}, u32[]{:S(2)}) %copy-start) | copy-done | bytes 524312
  2.4 0.0 copy-start.1
  2.4 1.0 %copy-done.1 = bf16[2,1,128,1024]{3,2,1,0:T(8,128)(2,1)S(1)} copy-done((bf16[2,1,128,1024]{3,2,1,0:T(8,128)(2,1)S(1)}, bf16[2,1,128,1024]{3,2,1,0:T(8,128)(2,1)}, u32[]{:S(2)}) %copy-start.1) | copy-done | bytes 524312
  3.4 0.0 copy-start.2
  3.4 0.8 copy-done.2
  4.2 0.0 copy-start.3
  4.2 0.8 copy-done.3
  5.1 76.8 %shard_map.84 = (bf16[2,128,1024]{2,1,0:T(8,128)(2,1)S(1)}, bf16[2,128,1024]{2,1,0:T(8,128)(2,1)S(1)}, bf16[2,128,128]{2,1,0:T(8,128)(2,1)S(1)}, bf16[2,128,128]{2,1,0:T(8,128)(2,1)S(1)}) custom-call(s32[256]{0:T(256)S(1)} %copy-done.4, bf16[2,128,1024]{2,1,0:T(8,128)(2,1)S(1)} %bitcast.18, bf16[2,128,128]{2,1,0:T(8,128)(2,1)S(1)} %bitcast.22, ...), custom_call_target="tpu_custom_call" | custom-call | tf_op jit(solution)/shard_map/pallas_call | solution.py:398
  81.9 0.8 copy.17
  82.7 0.8 copy.18
  83.5 0.6 copy.19
  84.1 0.6 copy.20
Async XLA Ops:
  0.6 0.7 copy-start.4
  1.3 1.0 %copy-start = (bf16[2,1,128,1024]{3,2,1,0:T(8,128)(2,1)S(1)}, bf16[2,1,128,1024]{3,2,1,0:T(8,128)(2,1)}, u32[]{:S(2)}) copy-start(bf16[2,1,128,1024]{3,2,1,0:T(8,128)(2,1)} %param.5) | copy-start | bytes 1572868
  2.4 1.0 %copy-start.1 = (bf16[2,1,128,1024]{3,2,1,0:T(8,128)(2,1)S(1)}, bf16[2,1,128,1024]{3,2,1,0:T(8,128)(2,1)}, u32[]{:S(2)}) copy-start(bf16[2,1,128,1024]{3,2,1,0:T(8,128)(2,1)} %param.8) | copy-start | bytes 1572868
  3.4 0.8 copy-start.2
  4.2 0.8 copy-start.3

commit v4 on v3

--- a/solution.py
+++ b/solution.py
@@ -18,7 +18,7 @@
 SCALE = 1.0 / math.sqrt(HD)
 EXP2_SCALE = SCALE * math.log2(math.e)
 UP, DOWN = 0, 1
-LAG = 2
+LAG = 4
 VMEM_LIMIT = 44 * 1024 * 1024
 
 
@@ -339,14 +339,12 @@
         lax.fori_loop(0, count, body, 0)
 
     def stage(time, carry):
+        @pl.when(time == LAG - 1)
+        def _():
+            send_own(1)
+
         for piece in range(2):
             now = time - LAG * piece
-            if piece == 1:
-
-                @pl.when(now == -1)
-                def _():
-                    send_own(1)
-
             @pl.when((now >= 0) & (now < RUN // 2))
             def _(piece=piece, now=now):
                 fetch_step(piece, now)

time: 85.1 us -> 88.2 us (1.036)
  Pallas kernels: 76.8 us -> 79.9 us
    pallas_call x1, Pallas kernels: 76.8 us -> 79.9 us  [local(): pl.pallas_call(functools.partial(kernel, runs), out_shape=[jax.ShapeDtype...]
where the time goes in v4:
time: 88.2 us; the launch traced here: 87.9 us
  Pallas kernels  79.9 us (91%)
  local copies, waits for them, and re-layouts  7.28 us (8%)
    pallas_call x1, Pallas kernels, local(): pl.pallas_call(functools.partial(kernel, runs), out_shape=[jax.ShapeDtype...  79.9 us
    unnamed x14, local copies, waits for them, and re-layouts  7.28 us

profile of v4, /device:TPU:256, one launch (start us, length us, event | category | flops | bytes accessed | tf_op | source)
XLA Modules:
  0.0 87.9 jit_solution(4501462550133098870)
XLA Ops:
  0.6 0.0 copy-start.4
  0.6 0.7 copy-done.4
  1.3 0.0 copy-start
  1.3 1.0 %copy-done = bf16[2,1,128,1024]{3,2,1,0:T(8,128)(2,1)S(1)} copy-done((bf16[2,1,128,1024]{3,2,1,0:T(8,128)(2,1)S(1)}, bf16[2,1,128,1024]{3,2,1,0:T(8,128)(2,1)}, u32[]{:S(2)}) %copy-start) | copy-done | bytes 524312
  2.4 0.0 copy-start.1
  2.4 1.0 %copy-done.1 = bf16[2,1,128,1024]{3,2,1,0:T(8,128)(2,1)S(1)} copy-done((bf16[2,1,128,1024]{3,2,1,0:T(8,128)(2,1)S(1)}, bf16[2,1,128,1024]{3,2,1,0:T(8,128)(2,1)}, u32[]{:S(2)}) %copy-start.1) | copy-done | bytes 524312
  3.4 0.0 copy-start.2
  3.4 0.8 copy-done.2
  4.2 0.0 copy-start.3
  4.2 0.8 copy-done.3
  5.1 79.9 %shard_map.84 = (bf16[2,128,1024]{2,1,0:T(8,128)(2,1)S(1)}, bf16[2,128,1024]{2,1,0:T(8,128)(2,1)S(1)}, bf16[2,128,128]{2,1,0:T(8,128)(2,1)S(1)}, bf16[2,128,128]{2,1,0:T(8,128)(2,1)S(1)}) custom-call(s32[256]{0:T(256)S(1)} %copy-done.4, bf16[2,128,1024]{2,1,0:T(8,128)(2,1)S(1)} %bitcast.18, bf16[2,128,128]{2,1,0:T(8,128)(2,1)S(1)} %bitcast.22, ...), custom_call_target="tpu_custom_call" | custom-call | tf_op jit(solution)/shard_map/pallas_call | solution.py:396
  85.0 0.8 copy.17
  85.8 0.8 copy.18
  86.6 0.6 copy.19
  87.2 0.6 copy.20
Async XLA Ops:
  0.6 0.7 copy-start.4
  1.3 1.0 %copy-start = (bf16[2,1,128,1024]{3,2,1,0:T(8,128)(2,1)S(1)}, bf16[2,1,128,1024]{3,2,1,0:T(8,128)(2,1)}, u32[]{:S(2)}) copy-start(bf16[2,1,128,1024]{3,2,1,0:T(8,128)(2,1)} %param.5) | copy-start | bytes 1572868
  2.4 1.0 %copy-start.1 = (bf16[2,1,128,1024]{3,2,1,0:T(8,128)(2,1)S(1)}, bf16[2,1,128,1024]{3,2,1,0:T(8,128)(2,1)}, u32[]{:S(2)}) copy-start(bf16[2,1,128,1024]{3,2,1,0:T(8,128)(2,1)} %param.8) | copy-start | bytes 1572868
  3.4 0.8 copy-start.2
  4.2 0.8 copy-start.3

commit v5 on v4

--- a/solution.py
+++ b/solution.py
@@ -18,7 +18,7 @@
 SCALE = 1.0 / math.sqrt(HD)
 EXP2_SCALE = SCALE * math.log2(math.e)
 UP, DOWN = 0, 1
-LAG = 4
+LAG = 1
 VMEM_LIMIT = 44 * 1024 * 1024
 
 

time: 88.2 us -> 84.1 us (0.954)
  the two profiles are of different devices: /device:TPU:256 before, /device:TPU:264 now
where the time goes in v5:
time: 84.1 us; the launch traced here: 83.8 us
  Pallas kernels  75.8 us (90%)
  local copies, waits for them, and re-layouts  7.28 us (9%)
    pallas_call x1, Pallas kernels, local(): pl.pallas_call(functools.partial(kernel, runs), out_shape=[jax.ShapeDtype...  75.8 us
    unnamed x14, local copies, waits for them, and re-layouts  7.28 us

profile of v5, /device:TPU:264, one launch (start us, length us, event | category | flops | bytes accessed | tf_op | source)
XLA Modules:
  0.0 83.8 jit_solution(4534253989201724562)
XLA Ops:
  0.6 0.0 copy-start.4
  0.6 0.7 copy-done.4
  1.3 0.0 copy-start
  1.3 1.0 %copy-done = bf16[2,1,128,1024]{3,2,1,0:T(8,128)(2,1)S(1)} copy-done((bf16[2,1,128,1024]{3,2,1,0:T(8,128)(2,1)S(1)}, bf16[2,1,128,1024]{3,2,1,0:T(8,128)(2,1)}, u32[]{:S(2)}) %copy-start) | copy-done | bytes 524312
  2.4 0.0 copy-start.1
  2.4 1.0 %copy-done.1 = bf16[2,1,128,1024]{3,2,1,0:T(8,128)(2,1)S(1)} copy-done((bf16[2,1,128,1024]{3,2,1,0:T(8,128)(2,1)S(1)}, bf16[2,1,128,1024]{3,2,1,0:T(8,128)(2,1)}, u32[]{:S(2)}) %copy-start.1) | copy-done | bytes 524312
  3.4 0.0 copy-start.2
  3.4 0.8 copy-done.2
  4.2 0.0 copy-start.3
  4.2 0.8 copy-done.3
  5.1 75.8 %shard_map.84 = (bf16[2,128,1024]{2,1,0:T(8,128)(2,1)S(1)}, bf16[2,128,1024]{2,1,0:T(8,128)(2,1)S(1)}, bf16[2,128,128]{2,1,0:T(8,128)(2,1)S(1)}, bf16[2,128,128]{2,1,0:T(8,128)(2,1)S(1)}) custom-call(s32[256]{0:T(256)S(1)} %copy-done.4, bf16[2,128,1024]{2,1,0:T(8,128)(2,1)S(1)} %bitcast.18, bf16[2,128,128]{2,1,0:T(8,128)(2,1)S(1)} %bitcast.22, ...), custom_call_target="tpu_custom_call" | custom-call | tf_op jit(solution)/shard_map/pallas_call | solution.py:396
  80.9 0.8 copy.17
  81.7 0.8 copy.18
  82.5 0.6 copy.19
  83.1 0.6 copy.20
Async XLA Ops:
  0.6 0.7 copy-start.4
  1.3 1.0 %copy-start = (bf16[2,1,128,1024]{3,2,1,0:T(8,128)(2,1)S(1)}, bf16[2,1,128,1024]{3,2,1,0:T(8,128)(2,1)}, u32[]{:S(2)}) copy-start(bf16[2,1,128,1024]{3,2,1,0:T(8,128)(2,1)} %param.5) | copy-start | bytes 1572868
  2.4 1.0 %copy-start.1 = (bf16[2,1,128,1024]{3,2,1,0:T(8,128)(2,1)S(1)}, bf16[2,1,128,1024]{3,2,1,0:T(8,128)(2,1)}, u32[]{:S(2)}) copy-start(bf16[2,1,128,1024]{3,2,1,0:T(8,128)(2,1)} %param.8) | copy-start | bytes 1572868
  3.4 0.8 %copy-start.2 = (bf16[2,1,128,128]{3,2,1,0:T(8,128)(2,1)S(1)}, bf16[2,1,128,128]{3,2,1,0:T(8,128)(2,1)}, u32[]{:S(2)}) copy-start(bf16[2,1,128,128]{3,2,1,0:T(8,128)(2,1)} %param.6) | copy-start | bytes 196612
  4.2 0.8 %copy-start.3 = (bf16[2,1,128,128]{3,2,1,0:T(8,128)(2,1)S(1)}, bf16[2,1,128,128]{3,2,1,0:T(8,128)(2,1)}, u32[]{:S(2)}) copy-start(bf16[2,1,128,128]{3,2,1,0:T(8,128)(2,1)} %param.7) | copy-start | bytes 196612
